TPU v7x, 128 devices: a whole 4x4x4 slice. The times are simulated.
128 devices in a mesh: seq: 16 (over z_hi, x, core), head: 8 (over z_lo, y).
Axes of the slice: x: 4, y: 4, z: 4 (z_hi: 2, z_lo: 2; z = z_hi * 2 + z_lo), core: 2. Of those that a mesh axis runs over, the one named last changes fastest.
Arguments:
- layer_input: bfloat16 [8192, 5376], P('seq'), may hold values from -6 to 6
- query: bfloat16 [8192, 4096], P('seq', 'head'), may hold values from -6 to 6
- keys: bfloat16 [8192, 2048], P('seq', 'head'), may hold values from -6 to 6
- values: bfloat16 [8192, 2048], P('seq', 'head'), may hold values from -6 to 6
- out_grad: bfloat16 [8192, 4096], P('seq', 'head'), may hold values from -6 to 6
- w_query: bfloat16 [5376, 4096], P(None, 'head'), may hold values from -0.078125 to 0.078125
- w_key: bfloat16 [5376, 2048], P(None, 'head'), may hold values from -0.078125 to 0.078125
- w_value: bfloat16 [5376, 2048], P(None, 'head'), may hold values from -0.078125 to 0.078125
- proof_lengths: int32 [16], replicated, may hold values from 1 to 2048, 8192 in all
Outputs:
- input_grad: bfloat16 [8192, 5376], P('seq', 'head')
- wq_grad: bfloat16 [5376, 4096], P('seq', 'head')
- wk_grad: bfloat16 [5376, 2048], P('seq', 'head')
- wv_grad: bfloat16 [5376, 2048], P('seq', 'head')
Inputs may be any that keep to these rules, and one draw needn't show every extreme that they name: `proof_lengths`: the lengths of the 16 proofs packed in order; they sum to 8192 and the longest has exactly 2048 tokens.
All inputs are finite; a program needn't handle non-finite values.
Results may differ from a plain program's by a relative error of at most 0.015.
Values may be sent and summed in bfloat16 or wider, within the bound.
A program may use at most 128 MiB of HBM per device.

v0:
```python
import jax
import jax.numpy as jnp
from jax import lax
from jax.sharding import PartitionSpec as P

D = 5376
H = 32
HD = 128
WINDOW = 1024


def shifted(block, axis, distance):
    devices = range(lax.axis_size(axis))
    route = [(i - distance, i) for i in devices if i - distance in devices]
    return lax.ppermute(block, axis, route)


def proof_index(positions, proof_lengths):
    lengths_sum = jnp.cumsum(proof_lengths)
    starts_at = lengths_sum - proof_lengths
    counted = jnp.sum((positions[:, None] >= starts_at[None, :]).astype(jnp.int32), axis=1)
    return counted - 1


def build_mask(query_pos, key_pos, query_seg, key_seg):
    before = key_pos[None, :] <= query_pos[:, None]
    inside = query_pos[:, None] - key_pos[None, :] < WINDOW
    present = key_pos[None, :] >= 0
    same_proof = query_seg[:, None] == key_seg[None, :]
    return before & inside & present & same_proof


def block_grads(q_block, k_block, v_block, g_block, pair_mask, score_scale):
    scores = (
        jnp.einsum("qkgd,lkd->kgql", q_block, k_block, preferred_element_type=jnp.float32)
        * score_scale
    )
    scores = jnp.where(pair_mask, scores, -1e30)
    row_max = jnp.max(scores, axis=-1, keepdims=True)
    weights_exp = jnp.where(pair_mask, jnp.exp(scores - row_max), 0.0)
    probs_full = weights_exp / jnp.sum(weights_exp, axis=-1, keepdims=True)
    probs_low = probs_full.astype(jnp.bfloat16)
    attn_out = jnp.einsum("kgql,lkd->qkgd", probs_low, v_block, preferred_element_type=jnp.float32)
    row_delta = jnp.einsum("qkgd,qkgd->kgq", g_block.astype(jnp.float32), attn_out)
    prob_grad = jnp.einsum("qkgd,lkd->kgql", g_block, v_block, preferred_element_type=jnp.float32)
    score_low = (probs_full * (prob_grad - row_delta[..., None])).astype(jnp.bfloat16)
    query_grad = (
        score_scale
        * jnp.einsum("kgql,lkd->qkgd", score_low, k_block, preferred_element_type=jnp.float32)
    ).astype(jnp.bfloat16)
    key_grad = score_scale * jnp.einsum(
        "kgql,qkgd->lkd", score_low, q_block, preferred_element_type=jnp.float32
    )
    value_grad = jnp.einsum(
        "kgql,qkgd->lkd", probs_low, g_block, preferred_element_type=jnp.float32
    )
    return (query_grad, key_grad, value_grad)


def input_product(layer_input, grads):
    return lax.dot_general(
        layer_input, grads, (((0,), (0,)), ((), ())), preferred_element_type=jnp.float32
    )


def transposed(left, right):
    return lax.dot_general(
        left, right, (((1,), (1,)), ((), ())), preferred_element_type=jnp.float32
    )


def on_device(layer_input, query, keys, values, out_grad, w_query, w_key, w_value, proof_lengths):
    row_count = query.shape[0]
    key_cols = keys.shape[1]
    query_cols = query.shape[1]
    kv_local = key_cols // HD
    groups = query_cols // key_cols
    score_scale = (D // H) ** (-0.5)
    halo_rows = min(row_count, WINDOW)
    halo_depth = max(WINDOW // row_count, 1)
    first_row = lax.axis_index("seq") * row_count
    edge_pair = jnp.stack([keys, values])
    arrived_blocks = []
    moving = edge_pair
    for hop_index in range(halo_depth):
        moving = shifted(moving, "seq", 1)
        arrived_blocks.insert(0, moving)
    ext_keys = jnp.concatenate([member[0] for member in arrived_blocks] + [keys], axis=0)
    ext_values = jnp.concatenate([member[1] for member in arrived_blocks] + [values], axis=0)
    query_pos = first_row + jnp.arange(row_count, dtype=jnp.int32)
    key_pos = first_row - WINDOW + jnp.arange(WINDOW + row_count, dtype=jnp.int32)
    query_seg = proof_index(query_pos, proof_lengths)
    key_seg = proof_index(key_pos, proof_lengths)
    block_rows = min(row_count, 512)
    span_rows = block_rows + WINDOW
    key_acc = jnp.zeros((WINDOW + row_count, kv_local, HD), jnp.float32)
    value_acc = jnp.zeros((WINDOW + row_count, kv_local, HD), jnp.float32)
    q_block = query.reshape(block_rows, kv_local, groups, HD)
    g_block = out_grad.reshape(block_rows, kv_local, groups, HD)
    k_block = ext_keys.reshape(span_rows, kv_local, HD)
    v_block = ext_values.reshape(span_rows, kv_local, HD)
    pair_mask = build_mask(query_pos, key_pos, query_seg, key_seg)
    q_grad, k_grad, v_grad = block_grads(q_block, k_block, v_block, g_block, pair_mask, score_scale)
    key_acc = key_acc.at[0:span_rows].add(k_grad)
    value_acc = value_acc.at[0:span_rows].add(v_grad)
    query_parts = q_grad.reshape(block_rows, query_cols)
    key_acc = key_acc.reshape(WINDOW + row_count, key_cols)
    value_acc = value_acc.reshape(WINDOW + row_count, key_cols)

    def halo_piece(distance):
        offset = (halo_depth - distance) * halo_rows
        return jnp.stack(
            [key_acc[offset : offset + halo_rows], value_acc[offset : offset + halo_rows]]
        )

    carried = halo_piece(halo_depth)
    for distance in range(halo_depth - 1, -1, -1):
        carried = shifted(carried.astype(jnp.bfloat16), "seq", -1).astype(carried.dtype)
        if distance > 0:
            carried = carried + halo_piece(distance)
    tail_start = row_count - halo_rows
    key_total = key_acc[WINDOW:].at[tail_start:].add(carried[0])
    value_total = value_acc[WINDOW:].at[tail_start:].add(carried[1])
    key_grad = key_total.astype(jnp.bfloat16)
    value_grad = value_total.astype(jnp.bfloat16)
    head_term = (
        transposed(query_parts, w_query)
        + transposed(key_grad, w_key)
        + transposed(value_grad, w_value)
    )
    input_grad = lax.psum_scatter(
        head_term.astype(jnp.bfloat16), "head", scatter_dimension=1, tiled=True
    )
    all_grads = jnp.concatenate([query_parts, key_grad, value_grad], axis=1)
    summed = lax.psum_scatter(
        input_product(layer_input, all_grads).astype(jnp.bfloat16),
        "seq",
        scatter_dimension=0,
        tiled=True,
    )
    wq_grad = summed[:, :query_cols]
    wk_grad = summed[:, query_cols : query_cols + key_cols]
    wv_grad = summed[:, query_cols + key_cols :]
    return (input_grad, wq_grad, wk_grad, wv_grad)


def solution(mesh):
    return jax.shard_map(
        on_device,
        mesh=mesh,
        in_specs=(
            P("seq", None),
            P("seq", "head"),
            P("seq", "head"),
            P("seq", "head"),
            P("seq", "head"),
            P(None, "head"),
            P(None, "head"),
            P(None, "head"),
            P(),
        ),
        out_specs=(P("seq", "head"), P("seq", "head"), P("seq", "head"), P("seq", "head")),
        check_vma=False,
    )
```

profile of v0, /device:TPU:1, one launch (start us, length us, event | category | flops | bytes accessed | tf_op | source)
XLA Modules:
  0.0 331.9 jit_solution(9683236239904864045)
XLA Ops:
  10.4 4.5 %collective-permute-start = (bf16[2,512,256]{1,2,0:T(8,128)(2,1)}, bf16[2,512,256]{1,2,0:T(8,128)(2,1)}, u32[]{:S(2)}, u32[]{:S(2)}) collective-permute-start(bf16[2,512,256]{1,2,0:T(8,128)(2,1)} %pad_maximum_fusion), channel_id=1, source_target_pairs={{0,8},{8,16},{16,24},{24,32},{32,40},{40,48},{48,56},{56,64},{64,7... | collective-permute-start | bytes 1572872 | tf_op jit(solution)/shard_map/ppermute | solution.py:15
  19.5 1.4 copy.91
  20.9 2.0 copy.121
  23.6 2.1 collective-permute-start.1
  25.7 3.2 fusion.11
  29.0 1.9 fusion.42
  30.8 1.8 copy.81
  32.6 1.8 copy.75
  34.4 1.9 fusion.41
  36.3 1.8 copy.80
  38.1 1.8 copy.74
  39.9 11.9 %fusion.43 = (f32[2,2,512]{2,1,0:T(2,128)S(1)}, f32[2,2,512,1536]{2,3,1,0:T(8,128)}) fusion(pred[512,1536]{0,1:T(8,128)(4,1)} %fusion.11, bf16[512,2,2,128]{0,3,2,1:T(8,128)(2,1)} %bitcast.120, bf16[512,2,128]{2,0,1:T(8,128)(2,1)} %copy.76, bf16[512,2,128]{2,0,1:T(8,128)(2,1)} %copy.75, bf16[512,2,128]{2,0,1:T(8,128)(2,1)} %copy.74), kind=kOutput, calls=%fused_computation.68 | convolution fusion | flops 823395840 | bytes 14688256 | tf_op jit(solution)/shard_map/sub | solution.py:40
  51.8 9.1 %fusion.8 = bf16[2,2,512,1536]{2,3,1,0:T(8,128)(2,1)} fusion(f32[2,2,512,1536]{2,3,1,0:T(8,128)} %get-tuple-element.113, f32[2,2,512]{2,1,0:T(2,128)S(1)} %get-tuple-element.112), kind=kLoop, calls=%fused_computation.14 | loop fusion | flops 6291456 | bytes 18882560 | tf_op jit(solution)/shard_map/convert_element_type | solution.py:42
  60.8 6.2 %convolution_bitcast_fusion = f32[1536,2,128]{0,2,1:T(8,128)} fusion(bf16[2,2,512,1536]{2,3,1,0:T(8,128)(2,1)} %fusion.8, bf16[512,2,2,128]{0,3,2,1:T(8,128)(2,1)S(1)} %copy-done.4), kind=kOutput, calls=%fused_computation.19 | convolution fusion | flops 805306368 | bytes 8388608 | tf_op jit(solution)/shard_map/kgql,qkgd->lkd/dot_general | solution.py:54
  67.1 2.1 convolution_bitcast_fusion.2
  69.2 2.3 copy.104
  71.4 3.5 %multiply_reduce_fusion = f32[2,2,512]{1,0,2:T(2,128)} fusion(f32[2,2,512,128]{3,1,0,2:T(2,128)} %copy.104, bf16[512,2,2,128]{3,2,1,0:T(2,128)(2,1)S(1)} %reshape.218), kind=kLoop, calls=%fused_computation.34 | loop fusion | flops 784384 | bytes 1581056
  76.2 6.8 %fusion.2 = bf16[2,2,512,1536]{2,3,1,0:T(8,128)(2,1)S(1)} fusion(bf16[512,2,2,128]{0,3,2,1:T(8,128)(2,1)} %copy.91, f32[2,2,512]{2,1,0:T(2,128)S(1)} %copy.105, f32[2,2,512,1536]{2,3,1,0:T(8,128)} %get-tuple-element.113, f32[2,2,512]{2,1,0:T(2,128)S(1)} %get-tuple-element.112, bf16[512,2,128]{2,0,1:T(8,128)(2,1)S(1)} %copy.82, ...), kind=kOutput, calls=%fused_computation.3 | convolution fusion | flops 820248576 | bytes 20201472 | tf_op jit(solution)/shard_map/qkgd,lkd->kgql/dot_general | solution.py:45
  82.9 2.1 fusion.13
  85.3 3.1 collective-permute-start.2
  88.7 7.2 %collective-permute-done.2 = bf16[2,512,256]{1,2,0:T(8,128)(2,1)S(1)} collective-permute-done((bf16[2,512,256]{1,2,0:T(8,128)(2,1)S(1)}, bf16[2,512,256]{1,2,0:T(8,128)(2,1)S(1)}, u32[]{:S(2)}, u32[]{:S(2)}) %collective-permute-start.2) | collective-permute-done | bytes 524320 | tf_op jit(solution)/shard_map/ppermute | solution.py:15
  96.1 2.2 collective-permute-start.3
  99.4 7.4 %collective-permute-done.3 = bf16[2,512,256]{1,2,0:T(8,128)(2,1)S(1)} collective-permute-done((bf16[2,512,256]{1,2,0:T(8,128)(2,1)S(1)}, bf16[2,512,256]{1,2,0:T(8,128)(2,1)S(1)}, u32[]{:S(2)}, u32[]{:S(2)}) %collective-permute-start.3) | collective-permute-done | bytes 524320 | tf_op jit(solution)/shard_map/ppermute | solution.py:15
  107.3 9.4 %fusion.3 = bf16[5376,1024]{0,1:T(8,128)(2,1)} fusion(bf16[512,5376]{1,0:T(8,128)(2,1)S(1)} %bitcast.134, bf16[512,256]{0,1:T(8,128)(2,1)S(1)} %get-tuple-element.104, bf16[512,256]{0,1:T(8,128)(2,1)S(1)} %get-tuple-element.105, bf16[512,512]{0,1:T(8,128)(2,1)S(1)} %bitcast.130), kind=kOutput, calls=%fused_computation.8 | convolution fusion | flops 5645795328 | bytes 17563648 | tf_op jit(solution)/shard_map/dot_general | solution.py:61
  116.7 14.7 %copy.116 = bf16[5376,1024]{1,0:T(8,128)(2,1)} copy(bf16[5376,1024]{0,1:T(8,128)(2,1)} %fusion.3) | data formatting | bytes 22020096
  131.5 5.3 %fusion.44 = f32[512,5376]{0,1:T(8,128)S(1)} fusion(bf16[5376,512]{1,0:T(8,128)(2,1)} %param.30, bf16[512,512]{0,1:T(8,128)(2,1)} %bitcast.131), kind=kOutput, calls=%fused_computation.69 | convolution fusion | flops 2818572288 | bytes 17039360 | tf_op jit(solution)/shard_map/dot_general | solution.py:67
  136.8 5.6 %fusion.45 = f32[512,5376]{0,1:T(8,128)} fusion(bf16[5376,256]{1,0:T(8,128)(2,1)S(1)} %copy-done, bf16[512,256]{0,1:T(8,128)(2,1)S(1)} %get-tuple-element.105), kind=kOutput, calls=%fused_computation.70 | convolution fusion | flops 1409286144 | bytes 14024704 | tf_op jit(solution)/shard_map/dot_general | solution.py:67
  142.4 9.0 %add_convert_fusion = bf16[512,5376]{0,1:T(8,128)(2,1)} fusion(f32[512,5376]{0,1:T(8,128)S(1)} %fusion.44, f32[512,5376]{0,1:T(8,128)} %fusion.45, bf16[5376,256]{1,0:T(8,128)(2,1)} %param.32, bf16[512,256]{0,1:T(8,128)(2,1)S(1)} %get-tuple-element.104), kind=kOutput, calls=%fused_computation.7 | convolution fusion | flops 1417543680 | bytes 30539776 | tf_op jit(solution)/shard_map/dot_general | solution.py:67
  151.4 105.5 %reduce-scatter.7.cloned.1.call-done = bf16[336,1024]{1,0:T(8,128)(2,1)} async-done(((bf16[5376,1024]{1,0:T(8,128)(2,1)}), bf16[336,1024]{1,0:T(8,128)(2,1)}) %reduce-scatter.7.cloned.1.call-update) | async-done | bytes 688144
  256.9 1.7 slice.154
  258.6 1.8 fusion.40
  260.4 64.7 %reduce-scatter.5.cloned.1.call-done = bf16[512,672]{0,1:T(8,128)(2,1)} async-done(((bf16[512,5376]{0,1:T(8,128)(2,1)}), bf16[512,672]{0,1:T(8,128)(2,1)}) %reduce-scatter.5.cloned.1.call-update) | async-done | bytes 688144 | tf_op jit(solution)/shard_map/reduce_scatter | solution.py:131
  (61 shorter events, 11.8 us)
Async XLA Ops:
  7.2 129.6 %copy-start = (bf16[5376,256]{1,0:T(8,128)(2,1)S(1)}, bf16[5376,256]{1,0:T(8,128)(2,1)}, u32[]{:S(2)}) copy-start(bf16[5376,256]{1,0:T(8,128)(2,1)} %param.31) | copy-start | bytes 8257540
  7.2 249.7 %reduce-scatter.7.cloned.1.call-start = ((), (), s32[]{:S(2)}) async-start(), calls=%async_computation.3 | async-start | bytes 11698176
  10.4 13.2 %collective-permute-start = (bf16[2,512,256]{1,2,0:T(8,128)(2,1)}, bf16[2,512,256]{1,2,0:T(8,128)(2,1)}, u32[]{:S(2)}, u32[]{:S(2)}) collective-permute-start(bf16[2,512,256]{1,2,0:T(8,128)(2,1)} %pad_maximum_fusion), channel_id=1, source_target_pairs={{0,8},{8,16},{16,24},{24,32},{32,40},{40,48},{48,56},{56,64},{64,7... | collective-permute-start | bytes 1572872 | tf_op jit(solution)/shard_map/ppermute | solution.py:15
  14.9 3.2 copy-start.11
  23.6 10.8 %collective-permute-start.1 = (bf16[2,512,256]{1,2,0:T(8,128)(2,1)}, bf16[2,512,256]{1,2,0:T(8,128)(2,1)}, u32[]{:S(2)}, u32[]{:S(2)}) collective-permute-start(bf16[2,512,256]{1,2,0:T(8,128)(2,1)} %collective-permute-done), channel_id=1, source_target_pairs={{0,8},{8,16},{16,24},{24,32},{32,40},{40,48},{48,56},{56,64},{64,7... | collective-permute-start | bytes 1572872 | tf_op jit(solution)/shard_map/ppermute | solution.py:15
  51.8 9.1 %copy-start.4 = (bf16[512,2,2,128]{0,3,2,1:T(8,128)(2,1)S(1)}, bf16[512,2,2,128]{0,3,2,1:T(8,128)(2,1)}, u32[]{:S(2)}) copy-start(bf16[512,2,2,128]{0,3,2,1:T(8,128)(2,1)} %copy.91) | copy-start | bytes 1572868
  60.8 6.3 %copy-start.1 = (bf16[2,2,512,1536]{2,3,1,0:T(8,128)(2,1)S(1)}, bf16[2,2,512,1536]{2,3,1,0:T(8,128)(2,1)}, u32[]{:S(2)}) copy-start(bf16[2,2,512,1536]{2,3,1,0:T(8,128)(2,1)} %fusion.8) | copy-start | bytes 18874372
  60.8 6.3 %copy-start.5 = (bf16[512,2,128]{2,0,1:T(8,128)(2,1)S(1)}, bf16[512,2,128]{2,0,1:T(8,128)(2,1)}, u32[]{:S(2)}) copy-start(bf16[512,2,128]{2,0,1:T(8,128)(2,1)} %copy.81) | copy-start | bytes 786436
  60.8 6.3 %copy-start.6 = (bf16[512,2,128]{2,0,1:T(8,128)(2,1)S(1)}, bf16[512,2,128]{2,0,1:T(8,128)(2,1)}, u32[]{:S(2)}) copy-start(bf16[512,2,128]{2,0,1:T(8,128)(2,1)} %copy.80) | copy-start | bytes 786436
  76.1 6.8 %copy-start.3 = (bf16[512,512]{0,1:T(8,128)(2,1)S(1)}, bf16[512,512]{0,1:T(8,128)(2,1)}, u32[]{:S(2)}) copy-start(bf16[512,512]{0,1:T(8,128)(2,1)} %copy.121) | copy-start | bytes 1572868
  82.9 2.2 copy-start.2
  85.1 13.2 %copy-start.8 = (bf16[512,2,128]{2,0,1:T(8,128)(2,1)S(1)}, bf16[512,2,128]{2,0,1:T(8,128)(2,1)}, u32[]{:S(2)}) copy-start(bf16[512,2,128]{2,0,1:T(8,128)(2,1)} %copy.76) | copy-start | bytes 786436
  85.1 13.2 %copy-start.9 = (bf16[512,2,128]{2,0,1:T(8,128)(2,1)S(1)}, bf16[512,2,128]{2,0,1:T(8,128)(2,1)}, u32[]{:S(2)}) copy-start(bf16[512,2,128]{2,0,1:T(8,128)(2,1)} %copy.75) | copy-start | bytes 786436
  85.1 13.2 %copy-start.10 = (bf16[512,2,128]{2,0,1:T(8,128)(2,1)S(1)}, bf16[512,2,128]{2,0,1:T(8,128)(2,1)}, u32[]{:S(2)}) copy-start(bf16[512,2,128]{2,0,1:T(8,128)(2,1)} %copy.74) | copy-start | bytes 786436
  85.3 10.6 %collective-permute-start.2 = (bf16[2,512,256]{1,2,0:T(8,128)(2,1)S(1)}, bf16[2,512,256]{1,2,0:T(8,128)(2,1)S(1)}, u32[]{:S(2)}, u32[]{:S(2)}) collective-permute-start(bf16[2,512,256]{1,2,0:T(8,128)(2,1)S(1)} %pad_maximum_fusion.1), channel_id=1, source_target_pairs={{8,0},{16,8},{24,16},{32,24},{40,32},{48,40},{56,48},{64,56},{72,6... | collective-permute-start | bytes 1572872 | tf_op jit(solution)/shard_map/ppermute | solution.py:15
  95.9 11.3 %slice-start = ((s8[5505024]{0:T(1024)(128)(4,1)}), s8[4194304]{0:T(1024)(128)(4,1)S(1)}, s32[]{:S(2)}) async-start(s8[5505024]{0:T(1024)(128)(4,1)} %bitcast.133), calls=%async_computation.4 | async-start | bytes 8388608
  96.1 11.2 %slice-start.1 = ((s8[5505024]{0:T(1024)(128)(4,1)}), s8[1310720]{0:T(1024)(128)(4,1)S(1)}, s32[]{:S(2)}) async-start(s8[5505024]{0:T(1024)(128)(4,1)} %bitcast.133), calls=%async_computation.5 | async-start | bytes 2621440
  96.1 10.8 %collective-permute-start.3 = (bf16[2,512,256]{1,2,0:T(8,128)(2,1)S(1)}, bf16[2,512,256]{1,2,0:T(8,128)(2,1)S(1)}, u32[]{:S(2)}, u32[]{:S(2)}) collective-permute-start(bf16[2,512,256]{1,2,0:T(8,128)(2,1)S(1)} %fusion.17), channel_id=1, source_target_pairs={{8,0},{16,8},{24,16},{32,24},{40,32},{48,40},{56,48},{64,56},{72,6... | collective-permute-start | bytes 1572872 | tf_op jit(solution)/shard_map/ppermute | solution.py:15
  99.4 7.8 %copy-start.7 = (bf16[2,128,2,512]{3,1,2,0:T(8,128)(2,1)}, bf16[2,128,2,512]{3,1,2,0:T(8,128)(2,1)S(1)}, u32[]{:S(2)}) copy-start(bf16[2,128,2,512]{3,1,2,0:T(8,128)(2,1)S(1)} %fusion.16) | copy-start | bytes 1572868
  131.4 193.7 %reduce-scatter.5.cloned.1.call-start = ((), (), s32[]{:S(2)}) async-start(), calls=%async_computation.2 | async-start | bytes 6193152 | tf_op jit(solution)/shard_map/reduce_scatter | solution.py:131
Sparse Core Ops, SparseCore 0:
  131.5 125.2 reduce-scatter.6
  259.9 65.1 reduce-scatter.4
where the time goes:
time: 333 us; the launch traced here: 332 us
  waiting for transfers between devices  185 us (56%)
  matrix products  59.5 us (18%)
  local copies, waits for them, and re-layouts  41.7 us (13%)
  other arithmetic  19.5 us (6%)
  between operations  14.4 us (4%)
  starting transfers between devices  12 us (4%)
    unnamed x3, waiting for transfers between devices  105 us
    reduce_scatter x1, waiting for transfers between devices, on_device(): lax.psum_scatter(head_term.astype(jnp.bfloat16), 'head', scatter_dimensio...  64.7 us
    dot_general x3, matrix products, transposed(): lax.dot_general(left, right, (((1,), (1,)), ((), ())), preferred_element_...  19.9 us
    unnamed x32, local copies, waits for them, and re-layouts  19.4 us
    ppermute x4, waiting for transfers between devices, shifted(): return lax.ppermute(block, axis, route)  14.7 us
    sub x1, matrix products, block_grads(): weights_exp = jnp.where(pair_mask, jnp.exp(scores - row_max), 0.0)  11.9 us
    ppermute x4, starting transfers between devices, shifted(): return lax.ppermute(block, axis, route)  11.9 us
    dot_general x1, matrix products, input_product(): lax.dot_general(layer_input, grads, (((0,), (0,)), ((), ())), preferred_e...  9.38 us
  transfers between devices with their start and end apart: 6, of which 4 were waited for; matrix products, arithmetic and copies ran while one was open for 13% of the time, Pallas kernels for 0%

commit v1 on v0

v1 whole, which is shorter than its diff:
```python
import functools
import math

import jax
import jax.numpy as jnp
from jax import lax
from jax.experimental import pallas as pl
from jax.experimental.pallas import tpu as pltpu
from jax.sharding import PartitionSpec as P

D = 5376
H = 32
HD = 128
WINDOW = 1024
ROWS = 512
BLOCK = 128
SPAN = WINDOW + BLOCK
EXT = WINDOW + ROWS
SCALE = (D // H) ** -0.5
EXP2_SCALE = SCALE * math.log2(math.e)
F32 = jnp.float32
BF16 = jnp.bfloat16
PIECE = 336
MESH = pl.DeviceIdType.MESH

NN = (((1,), (0,)), ((), ()))
NT = (((1,), (1,)), ((), ()))


def dot(left, right, dims):
    return lax.dot_general(left, right, dims, preferred_element_type=F32)


def attention_kernel(
    lengths, q, g, k2, k1, k0, v2, v1, v0,
    dq, dk2, dk1, dk0, dv2, dv1, dv0,
    keys, values, bias, dk_acc, dv_acc,
):
    first_row = lax.axis_index("seq") * ROWS
    for part, (k, v) in enumerate(((k2, v2), (k1, v1), (k0, v0))):
        keys[part * ROWS:(part + 1) * ROWS, :] = k[...]
        values[part * ROWS:(part + 1) * ROWS, :] = v[...]
    dk_acc[...] = jnp.zeros_like(dk_acc)
    dv_acc[...] = jnp.zeros_like(dv_acc)

    def block(b, carry):
        i0 = pl.multiple_of(b * BLOCK, BLOCK)
        row = lax.broadcasted_iota(jnp.int32, (BLOCK, 1), 0)
        position = first_row + i0 + row
        start = jnp.zeros((BLOCK, 1), jnp.int32)
        proof_start = jnp.int32(0)
        for proof in range(lengths.shape[0]):
            start = jnp.maximum(start, jnp.where(position >= proof_start, proof_start, 0))
            proof_start = proof_start + lengths[proof]
        lowest = jnp.maximum(start, position - (WINDOW - 1))
        lowest = lowest - (first_row - WINDOW) - i0
        column = lax.broadcasted_iota(jnp.int32, (BLOCK, SPAN), 1)
        seen = (column >= lowest) & (column <= row + WINDOW)
        bias[...] = jnp.where(seen, 0.0, -1e30).astype(F32)
        rows = pl.ds(i0, BLOCK)
        span = pl.ds(i0, SPAN)
        for kv in range(2):
            lanes = slice(kv * HD, (kv + 1) * HD)
            heads = (slice(2 * kv * HD, (2 * kv + 1) * HD), slice((2 * kv + 1) * HD, (2 * kv + 2) * HD))
            q2 = jnp.concatenate([q[rows, h] for h in heads], axis=0)
            g2 = jnp.concatenate([g[rows, h] for h in heads], axis=0)
            k = keys[span, lanes]
            v = values[span, lanes]
            both = jnp.concatenate([bias[...], bias[...]], axis=0)
            scores = dot(q2, k, NT) + both
            top = jnp.max(scores, axis=1, keepdims=True)
            weight = jnp.exp2((scores - top) * EXP2_SCALE)
            probs = weight * (1.0 / jnp.sum(weight, axis=1, keepdims=True))
            low = probs.astype(BF16)
            prob_grad = dot(g2, v, NT)
            delta = jnp.sum(low.astype(F32) * prob_grad, axis=1, keepdims=True)
            score_low = (probs * (prob_grad - delta)).astype(BF16)
            query_grad = (dot(score_low, k, NN) * SCALE).astype(BF16)
            dq[rows, heads[0]] = query_grad[:BLOCK]
            dq[rows, heads[1]] = query_grad[BLOCK:]
            dk_acc[kv, :, span] += dot(q2.T, score_low, NN)
            dv_acc[kv, :, span] += dot(g2.T, low, NN)
        return carry

    lax.fori_loop(0, ROWS // BLOCK, block, 0)
    for kv in range(2):
        lanes = slice(kv * HD, (kv + 1) * HD)
        for part, (dk, dv) in enumerate(((dk2, dv2), (dk1, dv1), (dk0, dv0))):
            cols = slice(part * ROWS, (part + 1) * ROWS)
            dk[lanes, :] = (dk_acc[kv, :, cols] * SCALE).astype(dk.dtype)
            dv[lanes, :] = dv_acc[kv, :, cols].astype(dv.dtype)


def attention(lengths, q, g, k, v):
    vmem = pl.BlockSpec(memory_space=pltpu.VMEM)
    shape = (2 * HD, ROWS)
    sums = [jax.ShapeDtypeStruct(shape, t) for t in (BF16, BF16, F32)]
    return pl.pallas_call(
        attention_kernel,
        out_shape=[jax.ShapeDtypeStruct(q.shape, BF16)] + sums + sums,
        in_specs=[pl.BlockSpec(memory_space=pltpu.SMEM)] + [vmem] * 8,
        out_specs=[vmem] * 7,
        scratch_shapes=[
            pltpu.VMEM((EXT, 2 * HD), BF16),
            pltpu.VMEM((EXT, 2 * HD), BF16),
            pltpu.VMEM((BLOCK, SPAN), F32),
            pltpu.VMEM((2, HD, EXT), F32),
            pltpu.VMEM((2, HD, EXT), F32),
        ],
        compiler_params=pltpu.CompilerParams(vmem_limit_bytes=40 << 20),
        cost_estimate=pl.CostEstimate(flops=4 << 30, bytes_accessed=4 << 20, transcendentals=3 << 20),
        name="attention",
    )(lengths, q, g, *k, *v)


def coordinates():
    seq = lax.axis_index("seq")
    head = lax.axis_index("head")
    core, x, zh = seq % 2, (seq // 2) % 4, seq // 8
    y, zl = head % 4, head // 4

    def at(zh_, x_, core_, zl_, y_):
        return {"seq": zh_ * 8 + x_ * 2 + core_, "head": zl_ * 4 + y_}

    mate = at(zh, x, 1 - core, zl, y)
    right = (at(zh, (x + 1) % 4, core, zl, y), at(zh, x, core, zl, (y + 1) % 4))
    left = (at(zh, (x + 3) % 4, core, zl, y), at(zh, x, core, zl, (y + 3) % 4))
    across = (at(1 - zh, x, core, zl, y), at(zh, x, core, 1 - zl, y))
    return core, (x, y), (zh, zl), mate, right, left, across


def reduce_kernel(
    xt, wq, wk, wv, dq, dk, dv,
    out_h, out_q, out_k, out_v,
    x_own, wq_own, wk_own, wv_own, dq_all, dk_all, dv_all,
    part, relay, final, zland,
    load_sem, own_sem, mate_send, mate_recv, send_sem, recv_sem,
):
    core, place, depth, mate, right, left, across = coordinates()
    barrier = pltpu.get_barrier_semaphore()
    peers = (mate,) + right + left + across
    for peer in peers:
        pl.semaphore_signal(barrier, inc=1, device_id=peer, device_id_type=MESH)

    mine = pl.ds(pl.multiple_of(core * ROWS, ROWS), ROWS)
    other = 1 - core

    def target(axis, t):
        side, u = t // 4, t % 4
        off = 2 - u + (u // 2) * 3 - (u // 3) * 2
        z = (1 - depth[axis] + side) % 2
        return z * 4 + (place[axis] + off) % 4

    def weight_loads(t):
        h = target(1, t)
        return [
            pltpu.make_async_copy(wq.at[h], wq_own.at[t], load_sem.at[0, t]),
            pltpu.make_async_copy(wk.at[h], wk_own.at[t], load_sem.at[1, t]),
            pltpu.make_async_copy(wv.at[h], wv_own.at[t], load_sem.at[2, t]),
        ]

    def own_loads():
        return [
            pltpu.make_async_copy(dq, dq_all.at[mine, :], own_sem.at[0]),
            pltpu.make_async_copy(dk, dk_all.at[:, mine], own_sem.at[1]),
            pltpu.make_async_copy(dv, dv_all.at[:, mine], own_sem.at[2]),
        ]

    def x_load(t):
        s = target(0, t)
        return pltpu.make_async_copy(xt.at[2 * s + core], x_own.at[t, :, mine], load_sem.at[3, t])

    for copy in own_loads():
        copy.start()
    for t in range(8):
        for copy in weight_loads(t):
            copy.start()
        x_load(t).start()

    def remote(src, dst, send, recv, device):
        return pltpu.make_async_remote_copy(
            src_ref=src, dst_ref=dst, send_sem=send, recv_sem=recv,
            device_id=device, device_id_type=MESH,
        )

    def mate_grads():
        return [
            remote(dq, dq_all.at[mine, :], mate_send.at[0], mate_recv.at[0], mate),
            remote(dk, dk_all.at[:, mine], mate_send.at[1], mate_recv.at[1], mate),
            remote(dv, dv_all.at[:, mine], mate_send.at[2], mate_recv.at[2], mate),
        ]

    def mate_x(t):
        s = target(0, t)
        return remote(
            xt.at[2 * s + other], x_own.at[t, :, mine], mate_send.at[3 + t], mate_recv.at[3 + t], mate
        )

    pl.semaphore_wait(barrier, len(peers))
    for copy in mate_grads():
        copy.start()
    for t in range(8):
        mate_x(t).start()

    def hop(axis, n, src, dst, device):
        return remote(src, dst, send_sem.at[axis, n], recv_sem.at[axis, n], device)

    def opposite(axis, side, way):
        device = (right, left)[way][axis]
        return hop(axis, 7 * side + way, part.at[axis, side, 0, way], relay.at[axis, side, way], device)

    def plain(axis, side, way):
        device = (right, left)[way][axis]
        half = 1 - way
        return hop(
            axis, 7 * side + 2 + way, part.at[axis, side, 1 + way, half], final.at[axis, side, way, half], device
        )

    def summed(axis, side, way):
        device = (right, left)[way][axis]
        half = way
        return hop(
            axis, 7 * side + 4 + way, part.at[axis, side, 1 + way, half], final.at[axis, side, way, half], device
        )

    def crossing(axis, half):
        return hop(axis, (6, 13)[half], part.at[axis, 0, 3, half], zland.at[axis, half], across[axis])

    def forward(side):
        for axis in range(2):
            for way in range(2):
                opposite(axis, side, way).wait_recv()
                kept = part[axis, side, 1 + way, way].astype(F32)
                part[axis, side, 1 + way, way] = (kept + relay[axis, side, way].astype(F32)).astype(BF16)
                summed(axis, side, way).start()

    def collected(axis, side, half):
        total = part[axis, side, 3, half].astype(F32)
        return total + final[axis, side, 0, half].astype(F32) + final[axis, side, 1, half].astype(F32)

    for copy in own_loads():
        copy.wait()

    def step(t, carry):
        side, u = t // 4, t % 4
        for copy in weight_loads(t):
            copy.wait()
        x_load(t).wait()
        for half in range(2):
            product = dot(wq_own[t, half], dq_all[mine, :], NT)
            product += dot(wk_own[t, half], dk_all[:, mine], NN)
            product += dot(wv_own[t, half], dv_all[:, mine], NN)
            part[1, side, u, half] = product.astype(BF16)

        @pl.when(t == 0)
        def _():
            for copy in mate_grads():
                copy.wait()

        mate_x(t).wait()
        part[0, side, u, 0] = dot(x_own[t], dq_all[...], NN).astype(BF16)
        part[0, side, u, 1, :, : 2 * HD] = dot(x_own[t], dk_all[...], NT).astype(BF16)
        part[0, side, u, 1, :, 2 * HD:] = dot(x_own[t], dv_all[...], NT).astype(BF16)

        for now in range(2):
            @pl.when(t == 4 * now)
            def _():
                if now == 1:
                    forward(0)
                for axis in range(2):
                    for way in range(2):
                        opposite(axis, now, way).start()

            for way in range(2):
                @pl.when(t == 4 * now + 1 + way)
                def _():
                    for axis in range(2):
                        plain(axis, now, way).start()

        return carry

    lax.fori_loop(0, 8, step, 0)

    for axis in range(2):
        for way in range(2):
            plain(axis, 0, way).wait_recv()
            summed(axis, 0, way).wait_recv()
        for half in range(2):
            part[axis, 0, 3, half] = collected(axis, 0, half).astype(BF16)
            crossing(axis, half).start()
    forward(1)
    for axis in (1, 0):
        for way in range(2):
            plain(axis, 1, way).wait_recv()
            summed(axis, 1, way).wait_recv()
        for half in range(2):
            crossing(axis, half).wait_recv()
        result = [collected(axis, 1, half) + zland[axis, half].astype(F32) for half in range(2)]
        if axis == 1:
            out_h[...] = jnp.concatenate(result, axis=0).T.astype(BF16)
        else:
            out_q[...] = result[0].astype(BF16)
            out_k[...] = result[1][:, : 2 * HD].astype(BF16)
            out_v[...] = result[1][:, 2 * HD:].astype(BF16)
    for axis in range(2):
        for side in range(2):
            for way in range(2):
                opposite(axis, side, way).wait_send()
                plain(axis, side, way).wait_send()
                summed(axis, side, way).wait_send()
            crossing(axis, side).wait_send()


def reduced(xt, wq, wk, wv, dq, dk, dv):
    vmem = pl.BlockSpec(memory_space=pltpu.VMEM)
    anywhere = pl.BlockSpec(memory_space=pl.ANY)
    cols = 4 * HD
    dma = pltpu.SemaphoreType.DMA
    return pl.pallas_call(
        reduce_kernel,
        out_shape=[
            jax.ShapeDtypeStruct((ROWS, 2 * PIECE), BF16),
            jax.ShapeDtypeStruct((PIECE, cols), BF16),
            jax.ShapeDtypeStruct((PIECE, cols // 2), BF16),
            jax.ShapeDtypeStruct((PIECE, cols // 2), BF16),
        ],
        in_specs=[anywhere] * 4 + [vmem] * 3,
        out_specs=[vmem] * 4,
        scratch_shapes=[
            pltpu.VMEM((8, PIECE, 2 * ROWS), BF16),
            pltpu.VMEM((8, 2, PIECE, cols), BF16),
            pltpu.VMEM((8, 2, PIECE, cols // 2), BF16),
            pltpu.VMEM((8, 2, PIECE, cols // 2), BF16),
            pltpu.VMEM((2 * ROWS, cols), BF16),
            pltpu.VMEM((cols // 2, 2 * ROWS), BF16),
            pltpu.VMEM((cols // 2, 2 * ROWS), BF16),
            pltpu.VMEM((2, 2, 4, 2, PIECE, cols), BF16),
            pltpu.VMEM((2, 2, 2, PIECE, cols), BF16),
            pltpu.VMEM((2, 2, 2, 2, PIECE, cols), BF16),
            pltpu.VMEM((2, 2, PIECE, cols), BF16),
            dma((4, 8)),
            dma((3,)),
            dma((11,)),
            dma((11,)),
            dma((2, 14)),
            dma((2, 14)),
        ],
        compiler_params=pltpu.CompilerParams(
            collective_id=1, has_side_effects=True, vmem_limit_bytes=56 << 20
        ),
        name="reduce",
    )(xt, wq, wk, wv, dq, dk, dv)


def shifted(block, distance):
    devices = range(lax.axis_size("seq"))
    route = [(i - distance, i) for i in devices if i - distance in devices]
    return lax.ppermute(block, "seq", route)


def on_device(layer_input, query, keys, values, out_grad, w_query, w_key, w_value, proof_lengths):
    xt = layer_input.T.reshape(16, PIECE, ROWS)
    k = [shifted(keys, 2), shifted(keys, 1), keys]
    v = [shifted(values, 2), shifted(values, 1), values]
    dq, dk2, dk1, dk0, dv2, dv1, dv0 = attention(proof_lengths, query, out_grad, k, v)
    dk = dk0 + shifted(dk1, -1).astype(F32) + shifted(dk2, -2).astype(F32)
    dv = dv0 + shifted(dv1, -1).astype(F32) + shifted(dv2, -2).astype(F32)
    return tuple(
        reduced(
            xt,
            w_query.reshape(8, 2, PIECE, -1),
            w_key.reshape(8, 2, PIECE, -1),
            w_value.reshape(8, 2, PIECE, -1),
            dq,
            dk.astype(BF16),
            dv.astype(BF16),
        )
    )


def solution(mesh):
    return jax.shard_map(
        on_device,
        mesh=mesh,
        in_specs=(
            P("seq", None),
            P("seq", "head"),
            P("seq", "head"),
            P("seq", "head"),
            P("seq", "head"),
            P(None, "head"),
            P(None, "head"),
            P(None, "head"),
            P(),
        ),
        out_specs=(P("seq", "head"), P("seq", "head"), P("seq", "head"), P("seq", "head")),
        check_vma=False,
    )
```

time: 333 us -> 143 us (0.43)
  waiting for transfers between devices: 185 us -> 12.6 us
  Pallas kernels: 0 us -> 87.2 us
  matrix products: 59.5 us -> 0 us
  local copies, waits for them, and re-layouts: 41.7 us -> 20.9 us
  other arithmetic: 19.5 us -> 1.62 us
  between operations: 14.4 us -> 0.74 us
  starting transfers between devices: 12 us -> 19.3 us
    unnamed x3 -> x0, waiting for transfers between devices: 105 us -> none
    pallas_call x0 -> x2, Pallas kernels: none -> 87.2 us  [the longest x1 76 us: reduced(): pl.pallas_call(reduce_kernel, out_shape=[jax.ShapeDtypeStruct((ROWS, 2 *...]
    reduce_scatter x1 -> x0, waiting for transfers between devices: 64.7 us -> none  [on_device(): lax.psum_scatter(head_term.astype(jnp.bfloat16), 'head', scatter_dimensio...]
    dot_general x9 -> x0, matrix products: 47.6 us -> none  [the longest x3 19.9 us: transposed(): lax.dot_general(left, right, (((1,), (1,)), ((), ())), preferred_element_...]
    sub x1 -> x0, matrix products: 11.9 us -> none  [block_grads(): weights_exp = jnp.where(pair_mask, jnp.exp(scores - row_max), 0.0)]
    unnamed x32 -> x15, local copies, waits for them, and re-layouts: 19.4 us -> 10.3 us
    transpose x0 -> x1, local copies, waits for them, and re-layouts: none -> 8.31 us  [on_device(): xt = layer_input.T.reshape(16, PIECE, ROWS)]
    concatenate x6 -> x0, local copies, waits for them, and re-layouts: 8.19 us -> none  [the longest x3 4.43 us: on_device(): jnp.concatenate([member[0] for member in arrived_blocks] + [keys], axis=0)]
  transfers between devices with their start and end apart: 6 -> 8, of which waited for: 4 -> 4; matrix products, arithmetic and copies ran while one was open for 13% -> 6% of each run, Pallas kernels for 0% -> 0%
where the time goes in v1:
time: 143 us; the launch traced here: 142 us
  Pallas kernels  87.2 us (61%)
  local copies, waits for them, and re-layouts  20.9 us (15%)
  starting transfers between devices  19.3 us (13%)
  waiting for transfers between devices  12.6 us (9%)
  other arithmetic  1.62 us (1%)
    pallas_call x1, Pallas kernels, reduced(): pl.pallas_call(reduce_kernel, out_shape=[jax.ShapeDtypeStruct((ROWS, 2 *...  76 us
    ppermute x8, starting transfers between devices, shifted(): return lax.ppermute(block, 'seq', route)  19.3 us
    ppermute x8, waiting for transfers between devices, shifted(): return lax.ppermute(block, 'seq', route)  12.6 us
    pallas_call x1, Pallas kernels, attention(): pl.pallas_call(attention_kernel, out_shape=[jax.ShapeDtypeStruct(q.shape,...  11.1 us
    unnamed x15, local copies, waits for them, and re-layouts  10.3 us
    transpose x1, local copies, waits for them, and re-layouts, on_device(): xt = layer_input.T.reshape(16, PIECE, ROWS)  8.31 us
  transfers between devices with their start and end apart: 8, of which 4 were waited for; matrix products, arithmetic and copies ran while one was open for 6% of the time, Pallas kernels for 0%

profile of v1, /device:TPU:1, one launch (start us, length us, event | category | flops | bytes accessed | tf_op | source)
XLA Modules:
  0.0 142.4 jit_solution(10308257891310563690)
XLA Ops:
  0.6 3.9 %collective-permute-start = (bf16[512,256]{1,0:T(8,128)(2,1)}, bf16[512,256]{1,0:T(8,128)(2,1)S(1)}, u32[]{:S(2)}, u32[]{:S(2)}) collective-permute-start(bf16[512,256]{1,0:T(8,128)(2,1)} %k0.1), channel_id=1, source_target_pairs={{0,16},{8,24},{16,32},{24,40},{32,48},{40,56},{48,64},{56,72},{64,... | collective-permute-start | bytes 786440 | tf_op jit(solution)/shard_map/ppermute | solution.py:358
  4.6 3.9 %collective-permute-start.1 = (bf16[512,256]{1,0:T(8,128)(2,1)}, bf16[512,256]{1,0:T(8,128)(2,1)S(1)}, u32[]{:S(2)}, u32[]{:S(2)}) collective-permute-start(bf16[512,256]{1,0:T(8,128)(2,1)} %k0.1), channel_id=1, source_target_pairs={{0,8},{8,16},{16,24},{24,32},{32,40},{40,48},{48,56},{56,64},{64,7... | collective-permute-start | bytes 786440 | tf_op jit(solution)/shard_map/ppermute | solution.py:358
  8.5 2.8 %collective-permute-start.2 = (bf16[512,256]{1,0:T(8,128)(2,1)}, bf16[512,256]{1,0:T(8,128)(2,1)S(1)}, u32[]{:S(2)}, u32[]{:S(2)}) collective-permute-start(bf16[512,256]{1,0:T(8,128)(2,1)} %v0.1), channel_id=1, source_target_pairs={{0,16},{8,24},{16,32},{24,40},{32,48},{40,56},{48,64},{56,72},{64,... | collective-permute-start | bytes 786440 | tf_op jit(solution)/shard_map/ppermute | solution.py:358
  11.4 2.2 %collective-permute-start.3 = (bf16[512,256]{1,0:T(8,128)(2,1)}, bf16[512,256]{1,0:T(8,128)(2,1)S(1)}, u32[]{:S(2)}, u32[]{:S(2)}) collective-permute-start(bf16[512,256]{1,0:T(8,128)(2,1)} %v0.1), channel_id=1, source_target_pairs={{0,8},{8,16},{16,24},{24,32},{32,40},{40,48},{48,56},{56,64},{64,7... | collective-permute-start | bytes 786440 | tf_op jit(solution)/shard_map/ppermute | solution.py:358
  13.6 0.0 collective-permute-done.k2
  13.6 1.9 %collective-permute-done.1.k1 = bf16[512,256]{1,0:T(8,128)(2,1)S(1)} collective-permute-done((bf16[512,256]{1,0:T(8,128)(2,1)}, bf16[512,256]{1,0:T(8,128)(2,1)S(1)}, u32[]{:S(2)}, u32[]{:S(2)}) %collective-permute-start.1) | collective-permute-done | bytes 262176 | tf_op jit(solution)/shard_map/ppermute | solution.py:358
  15.5 3.9 %collective-permute-done.2.v2 = bf16[512,256]{1,0:T(8,128)(2,1)S(1)} collective-permute-done((bf16[512,256]{1,0:T(8,128)(2,1)}, bf16[512,256]{1,0:T(8,128)(2,1)S(1)}, u32[]{:S(2)}, u32[]{:S(2)}) %collective-permute-start.2) | collective-permute-done | bytes 262176 | tf_op jit(solution)/shard_map/ppermute | solution.py:358
  19.4 2.8 %collective-permute-done.3.v1 = bf16[512,256]{1,0:T(8,128)(2,1)S(1)} collective-permute-done((bf16[512,256]{1,0:T(8,128)(2,1)}, bf16[512,256]{1,0:T(8,128)(2,1)S(1)}, u32[]{:S(2)}, u32[]{:S(2)}) %collective-permute-start.3) | collective-permute-done | bytes 262176 | tf_op jit(solution)/shard_map/ppermute | solution.py:358
  22.2 1.0 copy-done.1
  23.3 1.0 copy-done.2
  24.3 0.9 copy-done.3
  25.3 0.9 copy-done.4
  26.2 0.7 copy-done.5
  26.9 11.1 %attention.1 = (bf16[512,512]{1,0:T(8,128)(2,1)S(1)}, bf16[256,512]{1,0:T(8,128)(2,1)S(1)}, bf16[256,512]{1,0:T(8,128)(2,1)S(1)}, f32[256,512]{1,0:T(8,128)S(1)}...) custom-call(s32[16]{0:T(128)S(1)} %copy-done.5, ...), custom_call_target="tpu_custom_call" | custom-call | flops 4294967296 | bytes 4194304 | tf_op jit(solution)/shard_map/attention/pallas_call | solution.py:98
  38.0 0.0 copy-start
  38.0 0.8 copy-done
  38.8 1.9 %collective-permute-start.4 = (bf16[256,512]{1,0:T(8,128)(2,1)S(1)}, bf16[256,512]{1,0:T(8,128)(2,1)S(1)}, u32[]{:S(2)}, u32[]{:S(2)}) collective-permute-start(bf16[256,512]{1,0:T(8,128)(2,1)S(1)} %get-tuple-element.13), channel_id=1, source_target_pairs={{8,0},{16,8},{24,16},{32,24},{40,32},{48,40},{56,48},{64,56},{72,6... | collective-permute-start | bytes 786440 | tf_op jit(solution)/shard_map/ppermute | solution.py:358
  40.7 1.3 collective-permute-start.5
  42.0 1.9 %collective-permute-start.6 = (bf16[256,512]{1,0:T(8,128)(2,1)S(1)}, bf16[256,512]{1,0:T(8,128)(2,1)S(1)}, u32[]{:S(2)}, u32[]{:S(2)}) collective-permute-start(bf16[256,512]{1,0:T(8,128)(2,1)S(1)} %get-tuple-element.16), channel_id=1, source_target_pairs={{8,0},{16,8},{24,16},{32,24},{40,32},{48,40},{56,48},{64,56},{72,6... | collective-permute-start | bytes 786440 | tf_op jit(solution)/shard_map/ppermute | solution.py:358
  44.0 1.3 collective-permute-start.7
  45.3 8.3 %copy.13 = bf16[5376,512]{1,0:T(8,128)(2,1)} copy(bf16[5376,512]{0,1:T(8,128)(2,1)} %bitcast.6) | data formatting | bytes 11010048 | tf_op jit(solution)/shard_map/transpose | solution.py:362
  53.6 0.0 collective-permute-done.4
  53.6 0.0 collective-permute-done.5
  53.6 0.8 add_convert_fusion.1.dk
  54.4 4.0 %collective-permute-done.6 = bf16[256,512]{1,0:T(8,128)(2,1)S(1)} collective-permute-done((bf16[256,512]{1,0:T(8,128)(2,1)S(1)}, bf16[256,512]{1,0:T(8,128)(2,1)S(1)}, u32[]{:S(2)}, u32[]{:S(2)}) %collective-permute-start.6) | collective-permute-done | bytes 262176 | tf_op jit(solution)/shard_map/ppermute | solution.py:358
  58.4 0.0 collective-permute-done.7
  58.4 0.8 add_convert_fusion.dv
  59.2 76.0 %reduce.1 = (bf16[512,672]{1,0:T(8,128)(2,1)}, bf16[336,512]{1,0:T(8,128)(2,1)}, bf16[336,256]{1,0:T(8,128)(2,1)}, bf16[336,256]{1,0:T(8,128)(2,1)}) custom-call(bf16[16,336,512]{2,1,0:T(8,128)(2,1)} %bitcast.5, bf16[8,2,336,512]{3,2,1,0:T(8,128)(2,1)} %bitcast.7, bf16[8,2,336,256]{3,2,1,0:T(8,128)(2,1)} %bitcast.8, bf16[8,2,336,256]{3,2,1,0:T(8,128)(2,1)} %bitcast.9, ...), custom_call_target="tpu_custom_call" | custom-call | tf_op jit(solution)/shard_map/reduce/pallas_call | solution.py:319
  135.2 2.2 %copy.14 = bf16[512,672]{0,1:T(8,128)(2,1)} copy(bf16[512,672]{1,0:T(8,128)(2,1)} %get-tuple-element.18) | data formatting | bytes 1376256 | tf_op jit(solution)/shard_map/reduce/pallas_call | solution.py:319
  137.4 1.7 %copy.18 = bf16[336,512]{1,0:T(8,128)(2,1)} copy(bf16[336,512]{1,0:T(8,128)(2,1)} %get-tuple-element.27) | data formatting | bytes 688128
  139.2 1.6 %copy.19 = bf16[336,256]{1,0:T(8,128)(2,1)} copy(bf16[336,256]{1,0:T(8,128)(2,1)} %get-tuple-element.28) | data formatting | bytes 344064
  140.8 1.6 %copy.20 = bf16[336,256]{1,0:T(8,128)(2,1)} copy(bf16[336,256]{1,0:T(8,128)(2,1)} %get-tuple-element.29) | data formatting | bytes 344064
  (5 shorter events, 0.0 us)
Async XLA Ops:
  0.6 13.0 %collective-permute-start = (bf16[512,256]{1,0:T(8,128)(2,1)}, bf16[512,256]{1,0:T(8,128)(2,1)S(1)}, u32[]{:S(2)}, u32[]{:S(2)}) collective-permute-start(bf16[512,256]{1,0:T(8,128)(2,1)} %k0.1), channel_id=1, source_target_pairs={{0,16},{8,24},{16,32},{24,40},{32,48},{40,56},{48,64},{56,72},{64,... | collective-permute-start | bytes 786440 | tf_op jit(solution)/shard_map/ppermute | solution.py:358
  4.6 10.9 %collective-permute-start.1 = (bf16[512,256]{1,0:T(8,128)(2,1)}, bf16[512,256]{1,0:T(8,128)(2,1)S(1)}, u32[]{:S(2)}, u32[]{:S(2)}) collective-permute-start(bf16[512,256]{1,0:T(8,128)(2,1)} %k0.1), channel_id=1, source_target_pairs={{0,8},{8,16},{16,24},{24,32},{32,40},{40,48},{48,56},{56,64},{64,7... | collective-permute-start | bytes 786440 | tf_op jit(solution)/shard_map/ppermute | solution.py:358
  8.5 10.9 %collective-permute-start.2 = (bf16[512,256]{1,0:T(8,128)(2,1)}, bf16[512,256]{1,0:T(8,128)(2,1)S(1)}, u32[]{:S(2)}, u32[]{:S(2)}) collective-permute-start(bf16[512,256]{1,0:T(8,128)(2,1)} %v0.1), channel_id=1, source_target_pairs={{0,16},{8,24},{16,32},{24,40},{32,48},{40,56},{48,64},{56,72},{64,... | collective-permute-start | bytes 786440 | tf_op jit(solution)/shard_map/ppermute | solution.py:358
  11.4 10.8 %collective-permute-start.3 = (bf16[512,256]{1,0:T(8,128)(2,1)}, bf16[512,256]{1,0:T(8,128)(2,1)S(1)}, u32[]{:S(2)}, u32[]{:S(2)}) collective-permute-start(bf16[512,256]{1,0:T(8,128)(2,1)} %v0.1), channel_id=1, source_target_pairs={{0,8},{8,16},{16,24},{24,32},{32,40},{40,48},{48,56},{56,64},{64,7... | collective-permute-start | bytes 786440 | tf_op jit(solution)/shard_map/ppermute | solution.py:358
  22.2 1.0 copy-start.1
  23.3 1.0 copy-start.2
  24.3 0.9 copy-start.3
  25.3 0.9 copy-start.4
  26.2 0.7 copy-start.5
  38.0 0.8 copy-start
  38.8 14.8 %collective-permute-start.4 = (bf16[256,512]{1,0:T(8,128)(2,1)S(1)}, bf16[256,512]{1,0:T(8,128)(2,1)S(1)}, u32[]{:S(2)}, u32[]{:S(2)}) collective-permute-start(bf16[256,512]{1,0:T(8,128)(2,1)S(1)} %get-tuple-element.13), channel_id=1, source_target_pairs={{8,0},{16,8},{24,16},{32,24},{40,32},{48,40},{56,48},{64,56},{72,6... | collective-permute-start | bytes 786440 | tf_op jit(solution)/shard_map/ppermute | solution.py:358
  40.7 12.8 %collective-permute-start.5 = (bf16[256,512]{1,0:T(8,128)(2,1)S(1)}, bf16[256,512]{1,0:T(8,128)(2,1)S(1)}, u32[]{:S(2)}, u32[]{:S(2)}) collective-permute-start(bf16[256,512]{1,0:T(8,128)(2,1)S(1)} %get-tuple-element.14), channel_id=1, source_target_pairs={{16,0},{24,8},{32,16},{40,24},{48,32},{56,40},{64,48},{72,56},{80,... | collective-permute-start | bytes 786440 | tf_op jit(solution)/shard_map/ppermute | solution.py:358
  42.0 16.3 %collective-permute-start.6 = (bf16[256,512]{1,0:T(8,128)(2,1)S(1)}, bf16[256,512]{1,0:T(8,128)(2,1)S(1)}, u32[]{:S(2)}, u32[]{:S(2)}) collective-permute-start(bf16[256,512]{1,0:T(8,128)(2,1)S(1)} %get-tuple-element.16), channel_id=1, source_target_pairs={{8,0},{16,8},{24,16},{32,24},{40,32},{48,40},{56,48},{64,56},{72,6... | collective-permute-start | bytes 786440 | tf_op jit(solution)/shard_map/ppermute | solution.py:358
  44.0 14.4 %collective-permute-start.7 = (bf16[256,512]{1,0:T(8,128)(2,1)S(1)}, bf16[256,512]{1,0:T(8,128)(2,1)S(1)}, u32[]{:S(2)}, u32[]{:S(2)}) collective-permute-start(bf16[256,512]{1,0:T(8,128)(2,1)S(1)} %get-tuple-element.17), channel_id=1, source_target_pairs={{16,0},{24,8},{32,16},{40,24},{48,32},{56,40},{64,48},{72,56},{80,... | collective-permute-start | bytes 786440 | tf_op jit(solution)/shard_map/ppermute | solution.py:358

commit v2 on v0

v2 whole, which is shorter than its diff:
```python
import math

import jax
import jax.numpy as jnp
from jax import lax
from jax.experimental import pallas as pl
from jax.experimental.pallas import tpu as pltpu
from jax.sharding import PartitionSpec as P

D = 5376
H = 32
HD = 128
WINDOW = 1024
ROWS = 512
BLOCK = 128
SPAN = WINDOW + BLOCK
EXT = WINDOW + ROWS
SCALE = (D // H) ** -0.5
EXP2_SCALE = SCALE * math.log2(math.e)
F32 = jnp.float32
BF16 = jnp.bfloat16
PIECE = 336
CUT = 176
COLS = 512
MESH = pl.DeviceIdType.MESH

NN = (((1,), (0,)), ((), ()))
NT = (((1,), (1,)), ((), ()))

WEIGHT, INPUT = 0, 1
WAY_ROWS = (slice(0, CUT), slice(CUT, PIECE))


def dot(left, right, dims):
    return lax.dot_general(left, right, dims, preferred_element_type=F32)


def row_bias(lengths, first_row, i0):
    row = lax.broadcasted_iota(jnp.int32, (BLOCK, 1), 0)
    position = first_row + i0 + row
    start = jnp.zeros((BLOCK, 1), jnp.int32)
    proof_start = jnp.int32(0)
    for proof in range(lengths.shape[0]):
        start = jnp.maximum(start, jnp.where(position >= proof_start, proof_start, 0))
        proof_start = proof_start + lengths[proof]
    lowest = jnp.maximum(start, position - (WINDOW - 1))
    lowest = lowest - (first_row - WINDOW) - i0
    column = lax.broadcasted_iota(jnp.int32, (BLOCK, SPAN), 1)
    seen = (column >= lowest) & (column <= row + WINDOW)
    return jnp.where(seen, 0.0, -1e30).astype(F32)


def step_kernel(
    lengths, x, q_in, g_in, k_in, v_in, wq_in, wk_in, wv_in,
    out_h, out_q, out_kv,
    x_nat, xt, x_mate, q, g, keys, values, wq, wkv, bias, dk_acc, dv_acc,
    dq, dq_mate, dkv, dkv_mate, halo_out, halo_in,
    part, relay, final, zland, zrelay,
    load_sem, kv_send, kv_recv, gh_send, gh_recv, mate_send, mate_recv, send_sem, recv_sem,
):
    seq = lax.axis_index("seq")
    head = lax.axis_index("head")
    core, px, zh = seq % 2, (seq // 2) % 4, seq // 8
    py, zl = head % 4, head // 4
    zz = zh * 2 + zl

    def at(z_, x_, core_, y_):
        return {"seq": (z_ // 2) * 8 + x_ * 2 + core_, "head": (z_ % 2) * 4 + y_}

    mate = at(zz, px, 1 - core, py)
    right = (at(zz, (px + 1) % 4, core, py), at(zz, px, core, (py + 1) % 4))
    left = (at(zz, (px + 3) % 4, core, py), at(zz, px, core, (py + 3) % 4))
    above = at((zz + 1) % 4, px, core, py)
    below = at((zz + 3) % 4, px, core, py)
    beside = at(zh * 2 + 1 - zl, px, core, py)
    later = [{"seq": (seq + n) % 16, "head": head} for n in (1, 2)]
    earlier = [{"seq": (seq + 16 - n) % 16, "head": head} for n in (1, 2)]
    place, depth = (px, py), (zh, zl)

    barrier = pltpu.get_barrier_semaphore()
    peers = tuple(later) + tuple(earlier) + right + left + (above, below)
    for peer in peers:
        pl.semaphore_signal(barrier, inc=1, device_id=peer, device_id_type=MESH)

    places = (
        (q_in, q),
        (g_in, g),
        (k_in, keys.at[WINDOW:EXT, :]),
        (v_in, values.at[WINDOW:EXT, :]),
        (x, x_nat),
        (wq_in, wq),
        (wk_in, wkv.at[:, :, : 2 * HD]),
        (wv_in, wkv.at[:, :, 2 * HD:]),
    )

    def load(n):
        return pltpu.make_async_copy(*places[n], load_sem.at[n])

    for n in range(8):
        load(n).start()

    def remote(src, dst, send, recv, device):
        return pltpu.make_async_remote_copy(
            src_ref=src, dst_ref=dst, send_sem=send, recv_sem=recv,
            device_id=device, device_id_type=MESH,
        )

    def kv_copy(kv, n, which):
        src, dst = ((k_in, keys), (v_in, values))[which]
        lanes = slice(kv * HD, (kv + 1) * HD)
        rows = slice(WINDOW - (n + 1) * ROWS, WINDOW - n * ROWS)
        return remote(
            src.at[:, lanes], dst.at[rows, lanes],
            kv_send.at[kv, n, which], kv_recv.at[kv, n, which], later[n],
        )

    def grad_copy(kv, n, which):
        return remote(
            halo_out.at[kv, n, which], halo_in.at[kv, n, which],
            gh_send.at[kv, n, which], gh_recv.at[kv, n, which], earlier[n],
        )

    def mate_copy(n, src, dst):
        return remote(src, dst, mate_send.at[n], mate_recv.at[n], mate)

    def block_rows(index):
        return pl.ds(pl.multiple_of(index * PIECE, 16), PIECE)

    def mate_x(j):
        return mate_copy(j, xt.at[block_rows(2 * j + 1 - core), :], x_mate.at[j])

    def mate_dq(kv):
        lanes = slice(kv * 2 * HD, (kv + 1) * 2 * HD)
        return mate_copy(8 + kv, dq.at[:, lanes], dq_mate.at[:, lanes])

    def mate_dkv():
        return mate_copy(10, dkv, dkv_mate)

    pl.semaphore_wait(barrier, len(peers))
    for kv in range(2):
        for which in range(2):
            for n in range(2):
                kv_copy(kv, n, which).start()

    load(4).wait()

    def transpose(n, carry):
        cols = pl.ds(pl.multiple_of(n * 256, 256), 256)
        xt[cols, :] = x_nat[:, cols].T
        return carry

    lax.fori_loop(0, D // 256, transpose, 0)
    for j in range(8):
        mate_x(j).start()

    first_row = seq * ROWS
    dk_acc[...] = jnp.zeros_like(dk_acc)
    dv_acc[...] = jnp.zeros_like(dv_acc)

    def make_bias(b, carry):
        bias[b] = row_bias(lengths, first_row, b * BLOCK)
        return carry

    lax.fori_loop(0, ROWS // BLOCK, make_bias, 0)
    for n in range(4):
        load(n).wait()

    def attend(kv, b):
        i0 = pl.multiple_of(b * BLOCK, BLOCK)
        rows, span = pl.ds(i0, BLOCK), pl.ds(i0, SPAN)
        lanes = slice(kv * HD, (kv + 1) * HD)
        heads = [slice(n * HD, (n + 1) * HD) for n in (2 * kv, 2 * kv + 1)]
        q2 = jnp.concatenate([q[rows, h] for h in heads], axis=0)
        g2 = jnp.concatenate([g[rows, h] for h in heads], axis=0)
        k, v = keys[span, lanes], values[span, lanes]
        both = jnp.concatenate([bias[b], bias[b]], axis=0)
        scores = dot(q2, k, NT) + both
        top = jnp.max(scores, axis=1, keepdims=True)
        weight = jnp.exp2((scores - top) * EXP2_SCALE)
        probs = weight * (1.0 / jnp.sum(weight, axis=1, keepdims=True))
        low = probs.astype(BF16)
        prob_grad = dot(g2, v, NT)
        delta = jnp.sum(low.astype(F32) * prob_grad, axis=1, keepdims=True)
        score_low = (probs * (prob_grad - delta)).astype(BF16)
        query_grad = (dot(score_low, k, NN) * SCALE).astype(BF16)
        dq[rows, heads[0]] = query_grad[:BLOCK]
        dq[rows, heads[1]] = query_grad[BLOCK:]
        dk_acc[kv, :, span] += dot(q2.T, score_low, NN)
        dv_acc[kv, :, span] += dot(g2.T, low, NN)

    for kv in range(2):
        for which in range(2):
            for n in range(2):
                kv_copy(kv, n, which).wait_recv()

        def pair(b, carry, kv=kv):
            attend(kv, 2 * b)
            attend(kv, 2 * b + 1)
            return carry

        lax.fori_loop(0, ROWS // BLOCK // 2, pair, 0)
        for n in (1, 0):
            cols = slice(WINDOW - (n + 1) * ROWS, WINDOW - n * ROWS)
            halo_out[kv, n, 0] = (dk_acc[kv, :, cols] * SCALE).astype(BF16)
            halo_out[kv, n, 1] = dv_acc[kv, :, cols].astype(BF16)
            for which in range(2):
                grad_copy(kv, n, which).start()
        mate_dq(kv).start()

    def hop(axis, unit, n, src, dst, device):
        return remote(src, dst, send_sem.at[axis, unit, n], recv_sem.at[axis, unit, n], device)

    def opposite(axis, unit, way):
        device = (right, left)[way][axis]
        rows = WAY_ROWS[way]
        return hop(axis, unit, way, part.at[axis, unit, 0, rows], relay.at[axis, unit, rows], device)

    def plain(axis, unit, way):
        device = (right, left)[way][axis]
        rows = WAY_ROWS[1 - way]
        return hop(
            axis, unit, 2 + way, part.at[axis, unit, 1 + way, rows], final.at[axis, unit, way, rows], device
        )

    def summed(axis, unit, way):
        device = (right, left)[way][axis]
        rows = WAY_ROWS[way]
        return hop(
            axis, unit, 4 + way, part.at[axis, unit, 1 + way, rows], final.at[axis, unit, way, rows], device
        )

    def crossing(axis, unit, way):
        rows = WAY_ROWS[way]
        slot = unit // 2 if axis == WEIGHT else unit
        src = part.at[axis, unit, 3, rows]
        if axis == WEIGHT:
            return hop(axis, unit, 6 + way, src, zrelay.at[slot, rows], (above, below)[way])
        return hop(axis, unit, 6 + way, src, zland.at[axis, slot, rows], beside)

    def onward(unit, way):
        rows = WAY_ROWS[way]
        slot = unit // 2
        return hop(
            WEIGHT, unit, 8 + way, zrelay.at[slot, rows], zland.at[WEIGHT, slot, rows], (above, below)[way]
        )

    def target(axis, side, u):
        off = 2 - u + (u // 2) * 3 - (u // 3) * 2
        z = (1 - depth[axis] + side) % 2
        return z * 4 + (place[axis] + off) % 4

    def make_weight(unit):
        side, half = unit % 2, unit // 2
        own, other, dims = ((dq, dq_mate, NN), (dkv, dkv_mate, NT))[half]

        def body(u, carry):
            j = target(WEIGHT, side, u)
            product = dot(xt[block_rows(2 * j + core), :], own[...], dims)
            product += dot(x_mate[j], other[...], dims)
            part[WEIGHT, unit, u] = product.astype(BF16)
            return carry

        lax.fori_loop(0, 4, body, 0)

    def make_input(unit):
        side, half = unit // 2, unit % 2

        def body(u, carry):
            j = target(INPUT, side, u) * 2 + half
            product = dot(wq[j], dq[...], NT)
            product += dot(wkv[j], dkv[...], NN)
            part[INPUT, unit, u] = product.astype(BF16)
            return carry

        lax.fori_loop(0, 4, body, 0)

    def send(axis, unit):
        for way in range(2):
            opposite(axis, unit, way).start()
        for way in range(2):
            plain(axis, unit, way).start()

    def forward(axis, unit):
        for way in range(2):
            opposite(axis, unit, way).wait_recv()
            rows = WAY_ROWS[way]
            kept = part[axis, unit, 1 + way, rows].astype(F32)
            part[axis, unit, 1 + way, rows] = (kept + relay[axis, unit, rows].astype(F32)).astype(BF16)
            summed(axis, unit, way).start()

    def collected(axis, unit):
        for way in range(2):
            plain(axis, unit, way).wait_recv()
            summed(axis, unit, way).wait_recv()
        total = part[axis, unit, 3].astype(F32)
        return total + final[axis, unit, 0].astype(F32) + final[axis, unit, 1].astype(F32)

    def cross(axis, unit):
        part[axis, unit, 3] = collected(axis, unit).astype(BF16)
        for way in range(2):
            crossing(axis, unit, way).start()

    def carry_on(unit):
        for way in range(2):
            crossing(WEIGHT, unit, way).wait_recv()
            onward(unit, way).start()

    def finished(axis, unit):
        total = collected(axis, unit)
        source = unit - 1 if axis == WEIGHT else unit - 2
        slot = source // 2 if axis == WEIGHT else source
        for way in range(2):
            if axis == WEIGHT:
                onward(source, way).wait_recv()
            else:
                crossing(axis, source, way).wait_recv()
        return (total + zland[axis, slot].astype(F32)).astype(BF16)

    for j in range(8):
        mate_x(j).wait_recv()
    for kv in range(2):
        mate_dq(kv).wait_recv()
    make_weight(0)
    send(WEIGHT, 0)
    make_weight(1)
    forward(WEIGHT, 0)
    send(WEIGHT, 1)

    for kv in range(2):
        for n in range(2):
            for which in range(2):
                grad_copy(kv, n, which).wait_recv()
        own = slice(WINDOW, EXT)
        halo = [halo_in[kv, 0, n].astype(F32) + halo_in[kv, 1, n].astype(F32) for n in range(2)]
        dkv[kv * HD:(kv + 1) * HD, :] = (dk_acc[kv, :, own] * SCALE + halo[0]).astype(BF16)
        dkv[(2 + kv) * HD:(3 + kv) * HD, :] = (dv_acc[kv, :, own] + halo[1]).astype(BF16)
    mate_dkv().start()
    for n in (5, 6, 7):
        load(n).wait()

    make_input(0)
    send(INPUT, 0)
    make_input(1)
    forward(WEIGHT, 1)
    forward(INPUT, 0)
    send(INPUT, 1)
    mate_dkv().wait_recv()
    make_weight(2)
    send(WEIGHT, 2)
    make_input(2)
    cross(WEIGHT, 0)
    forward(INPUT, 1)
    send(INPUT, 2)
    make_weight(3)
    forward(WEIGHT, 2)
    send(WEIGHT, 3)
    make_input(3)
    carry_on(0)
    cross(INPUT, 0)
    forward(INPUT, 2)
    send(INPUT, 3)
    forward(WEIGHT, 3)
    cross(WEIGHT, 2)
    cross(INPUT, 1)
    carry_on(2)
    forward(INPUT, 3)
    out_q[...] = finished(WEIGHT, 1)
    out_kv[...] = finished(WEIGHT, 3)
    out_h[:PIECE, :] = finished(INPUT, 2)
    out_h[PIECE:, :] = finished(INPUT, 3)

    for kv in range(2):
        mate_dq(kv).wait_send()
        for n in range(2):
            for which in range(2):
                kv_copy(kv, n, which).wait_send()
                grad_copy(kv, n, which).wait_send()
    for j in range(8):
        mate_x(j).wait_send()
    mate_dkv().wait_send()
    for axis in range(2):
        for unit in range(4):
            for way in range(2):
                opposite(axis, unit, way).wait_send()
                plain(axis, unit, way).wait_send()
                summed(axis, unit, way).wait_send()
                if axis == WEIGHT and unit % 2 == 0:
                    crossing(axis, unit, way).wait_send()
                    onward(unit, way).wait_send()
                if axis == INPUT and unit < 2:
                    crossing(axis, unit, way).wait_send()


def whole_step(lengths, x, q, g, k, v, wq, wk, wv):
    vmem = pl.BlockSpec(memory_space=pltpu.VMEM)
    anywhere = pl.BlockSpec(memory_space=pl.ANY)
    dma = pltpu.SemaphoreType.DMA
    piece = (PIECE, COLS)
    return pl.pallas_call(
        step_kernel,
        out_shape=[
            jax.ShapeDtypeStruct((2 * PIECE, ROWS), BF16),
            jax.ShapeDtypeStruct(piece, BF16),
            jax.ShapeDtypeStruct(piece, BF16),
        ],
        in_specs=[pl.BlockSpec(memory_space=pltpu.SMEM)] + [anywhere] * 8,
        out_specs=[vmem] * 3,
        scratch_shapes=[
            pltpu.VMEM((ROWS, D), BF16),
            pltpu.VMEM((D, ROWS), BF16),
            pltpu.VMEM((8, PIECE, ROWS), BF16),
            pltpu.VMEM((ROWS, COLS), BF16),
            pltpu.VMEM((ROWS, COLS), BF16),
            pltpu.VMEM((EXT, 2 * HD), BF16),
            pltpu.VMEM((EXT, 2 * HD), BF16),
            pltpu.VMEM((16, PIECE, COLS), BF16),
            pltpu.VMEM((16, PIECE, COLS), BF16),
            pltpu.VMEM((ROWS // BLOCK, BLOCK, SPAN), F32),
            pltpu.VMEM((2, HD, EXT), F32),
            pltpu.VMEM((2, HD, EXT), F32),
            pltpu.VMEM((ROWS, COLS), BF16),
            pltpu.VMEM((ROWS, COLS), BF16),
            pltpu.VMEM((COLS, ROWS), BF16),
            pltpu.VMEM((COLS, ROWS), BF16),
            pltpu.VMEM((2, 2, 2, HD, ROWS), BF16),
            pltpu.VMEM((2, 2, 2, HD, ROWS), BF16),
            pltpu.VMEM((2, 4, 4) + piece, BF16),
            pltpu.VMEM((2, 4) + piece, BF16),
            pltpu.VMEM((2, 4, 2) + piece, BF16),
            pltpu.VMEM((2, 2) + piece, BF16),
            pltpu.VMEM((2,) + piece, BF16),
            dma((8,)),
            dma((2, 2, 2)),
            dma((2, 2, 2)),
            dma((2, 2, 2)),
            dma((2, 2, 2)),
            dma((11,)),
            dma((11,)),
            dma((2, 4, 10)),
            dma((2, 4, 10)),
        ],
        compiler_params=pltpu.CompilerParams(
            collective_id=1, has_side_effects=True, vmem_limit_bytes=67043328
        ),
        name="step",
    )(lengths, x, q, g, k, v, wq, wk, wv)


def write_kernel(h, q, kv, out_h, out_q, out_k, out_v):
    out_h[...] = h[...].T
    out_q[...] = q[...]
    out_k[...] = kv[:, : 2 * HD]
    out_v[...] = kv[:, 2 * HD:]


def written(h, q, kv):
    vmem = pl.BlockSpec(memory_space=pltpu.VMEM)
    shapes = ((ROWS, 2 * PIECE), (PIECE, COLS), (PIECE, COLS // 2), (PIECE, COLS // 2))
    return pl.pallas_call(
        write_kernel,
        out_shape=[jax.ShapeDtypeStruct(shape, BF16) for shape in shapes],
        in_specs=[vmem] * 3,
        out_specs=[vmem] * 4,
        name="write",
    )(h, q, kv)


def on_device(layer_input, query, keys, values, out_grad, w_query, w_key, w_value, proof_lengths):
    weights = [w.reshape(16, PIECE, -1) for w in (w_query, w_key, w_value)]
    return tuple(written(*whole_step(proof_lengths, layer_input, query, out_grad, keys, values, *weights)))


def solution(mesh):
    return jax.shard_map(
        on_device,
        mesh=mesh,
        in_specs=(
            P("seq", None),
            P("seq", "head"),
            P("seq", "head"),
            P("seq", "head"),
            P("seq", "head"),
            P(None, "head"),
            P(None, "head"),
            P(None, "head"),
            P(),
        ),
        out_specs=(P("seq", "head"), P("seq", "head"), P("seq", "head"), P("seq", "head")),
        check_vma=False,
    )
```

time: 333 us -> 106 us (0.32)
  the two profiles are of different devices: /device:TPU:1 before, /device:TPU:6 now
where the time goes in v2:
time: 106 us
  Pallas kernels  103 us (97%)
  local copies, waits for them, and re-layouts  2.23 us (2%)
    pallas_call x1, Pallas kernels, whole_step(): pl.pallas_call(step_kernel, out_shape=[jax.ShapeDtypeStruct((2 * PIECE, R...  100 us
    pallas_call x1, Pallas kernels, written(): pl.pallas_call(write_kernel, out_shape=[jax.ShapeDtypeStruct(shape, BF16)...  2.61 us
    pallas_call x1, local copies, waits for them, and re-layouts, written(): pl.pallas_call(write_kernel, out_shape=[jax.ShapeDtypeStruct(shape, BF16)...  2.23 us

profile of v2, /device:TPU:6, one launch (start us, length us, event | category | flops | bytes accessed | tf_op | source)
XLA Modules:
  0.0 106.0 jit_solution(8549986142351244030)
XLA Ops:
  0.6 100.5 %step.1 = (bf16[672,512]{1,0:T(8,128)(2,1)}, bf16[336,512]{1,0:T(8,128)(2,1)}, bf16[336,512]{1,0:T(8,128)(2,1)}) custom-call(s32[16]{0:T(128)} %lengths.1, bf16[512,5376]{1,0:T(8,128)(2,1)} %x.1, bf16[512,512]{1,0:T(8,128)(2,1)} %q_in.1, bf16[512,512]{1,0:T(8,128)(2,1)} %g_in.1, bf16[512,256]{1,0:T(8,128)(2,1)} %k_in.1, bf16[512,256]{1,0:T(8,128)(2,1)} %v_in.1, ...), custom_call_target="tpu_custom_call" | custom-call | tf_op jit(solution)/shard_map/step/pallas_call | solution.py:399
  101.1 2.6 %write.1 = (bf16[512,672]{1,0:T(8,128)(2,1)}, bf16[336,512]{1,0:T(8,128)(2,1)}, bf16[336,256]{1,0:T(8,128)(2,1)}, bf16[336,256]{1,0:T(8,128)(2,1)}) custom-call(bf16[672,512]{1,0:T(8,128)(2,1)} %get-tuple-element.7.h, bf16[336,512]{1,0:T(8,128)(2,1)} %get-tuple-element.8.q, bf16[336,512]{1,0:T(8,128)(2,1)} %get-tuple-element.9.kv), custom_call_target="tpu_custom_call" | custom-call | tf_op jit(solution)/shard_map/write/pallas_call | solution.py:459
  103.7 2.2 %copy.13 = bf16[512,672]{0,1:T(8,128)(2,1)} copy(bf16[512,672]{1,0:T(8,128)(2,1)} %get-tuple-element.10) | data formatting | bytes 1376256 | tf_op jit(solution)/shard_map/write/pallas_call | solution.py:459

commit v3 on v2

--- a/solution.py
+++ b/solution.py
@@ -54,9 +54,10 @@
     lengths, x, q_in, g_in, k_in, v_in, wq_in, wk_in, wv_in,
     out_h, out_q, out_kv,
     x_nat, xt, x_mate, q, g, keys, values, wq, wkv, bias, dk_acc, dv_acc,
-    dq, dq_mate, dkv, dkv_mate, halo_out, halo_in,
-    part, relay, final, zland, zrelay,
-    load_sem, kv_send, kv_recv, gh_send, gh_recv, mate_send, mate_recv, send_sem, recv_sem,
+    dq, dq_mate, dkv, dkv_mate, halo_out, halo_in, mate_far,
+    part, relay, final, zland,
+    load_sem, kv_send, kv_recv, gh_send, gh_recv, mate_send, mate_recv,
+    send_sem, recv_sem,
 ):
     seq = lax.axis_index("seq")
     head = lax.axis_index("head")
@@ -67,18 +68,19 @@
     def at(z_, x_, core_, y_):
         return {"seq": (z_ // 2) * 8 + x_ * 2 + core_, "head": (z_ % 2) * 4 + y_}
 
+    far_z = (zz + 2) % 4
+    next_z, prev_z = (zz + 2 * (px // 3)) % 4, (zz + 2 * ((3 - px) // 3)) % 4
+    chip = zh * 4 + px
     mate = at(zz, px, 1 - core, py)
     right = (at(zz, (px + 1) % 4, core, py), at(zz, px, core, (py + 1) % 4))
     left = (at(zz, (px + 3) % 4, core, py), at(zz, px, core, (py + 3) % 4))
-    above = at((zz + 1) % 4, px, core, py)
-    below = at((zz + 3) % 4, px, core, py)
-    beside = at(zh * 2 + 1 - zl, px, core, py)
-    later = [{"seq": (seq + n) % 16, "head": head} for n in (1, 2)]
-    earlier = [{"seq": (seq + 16 - n) % 16, "head": head} for n in (1, 2)]
+    across = (at(far_z, px, core, py), at(zh * 2 + 1 - zl, px, core, py))
     place, depth = (px, py), (zh, zl)
 
     barrier = pltpu.get_barrier_semaphore()
-    peers = tuple(later) + tuple(earlier) + right + left + (above, below)
+    peers = [mate, right[1], left[1], across[0], across[1]]
+    for k in range(2):
+        peers += [at(zz, (px + 1) % 4, k, py), at(zz, (px + 3) % 4, k, py), at(far_z, 3 - px, k, py)]
     for peer in peers:
         pl.semaphore_signal(barrier, inc=1, device_id=peer, device_id_type=MESH)
 
@@ -96,7 +98,7 @@
     def load(n):
         return pltpu.make_async_copy(*places[n], load_sem.at[n])
 
-    for n in range(8):
+    for n in range(5):
         load(n).start()
 
     def remote(src, dst, send, recv, device):
@@ -105,19 +107,47 @@
             device_id=device, device_id_type=MESH,
         )
 
-    def kv_copy(kv, n, which):
-        src, dst = ((k_in, keys), (v_in, values))[which]
-        lanes = slice(kv * HD, (kv + 1) * HD)
-        rows = slice(WINDOW - (n + 1) * ROWS, WINDOW - n * ROWS)
+    def head_lanes(kv):
+        return slice(kv * HD, (kv + 1) * HD)
+
+    def kv_remote(kv, slot, which, src, rows, send, device):
+        dst = (keys, values)[which].at[rows, head_lanes(kv)]
+        return remote(src, dst, kv_send.at[kv, send, which], kv_recv.at[kv, slot, which], device)
+
+    def kv_source(kv, which):
+        return (k_in, v_in)[which].at[:, head_lanes(kv)]
+
+    core_rows = pl.ds(pl.multiple_of(core * ROWS, ROWS), ROWS)
+    near, far = slice(ROWS, WINDOW), slice(0, ROWS)
+
+    def kv_next(kv, which):
+        device = at(next_z, (px + 1) % 4, 0, py)
+        dst = (keys, values)[which].at[core_rows, head_lanes(kv)]
         return remote(
-            src.at[:, lanes], dst.at[rows, lanes],
-            kv_send.at[kv, n, which], kv_recv.at[kv, n, which], later[n],
+            kv_source(kv, which), dst, kv_send.at[kv, 0, which], kv_recv.at[kv, core, which], device
         )
 
-    def grad_copy(kv, n, which):
+    def kv_mate(kv, which):
+        return kv_remote(kv, 1, which, kv_source(kv, which), near, 1, mate)
+
+    def kv_share(kv, which):
+        src = (keys, values)[which].at[near, head_lanes(kv)]
+        return kv_remote(kv, 0, which, src, far, 2, mate)
+
+    def kv_arrived(kv, slot, which):
+        kv_remote(kv, slot, which, kv_source(kv, which), (far, near)[slot], 0, mate).wait_recv()
+
+    def grad_mate(kv, n, which):
+        dst = halo_in.at[kv, 0, which] if n == 0 else mate_far.at[kv, which]
         return remote(
-            halo_out.at[kv, n, which], halo_in.at[kv, n, which],
-            gh_send.at[kv, n, which], gh_recv.at[kv, n, which], earlier[n],
+            halo_out.at[kv, n, which], dst, gh_send.at[kv, n, which], gh_recv.at[kv, 2 * n, which], mate
+        )
+
+    def grad_prev(kv, n, which):
+        device = at(prev_z, (px + 3) % 4, 1 - n, py)
+        return remote(
+            halo_out.at[kv, n, which], halo_in.at[kv, 1, which],
+            gh_send.at[kv, n, which], gh_recv.at[kv, 1, which], device,
         )
 
     def mate_copy(n, src, dst):
@@ -136,11 +166,42 @@
     def mate_dkv():
         return mate_copy(10, dkv, dkv_mate)
 
+    first_core, second_core = core == 0, core == 1
+    has_prev, has_next = chip > 0, chip < 7
+    both = range(2)
+
     pl.semaphore_wait(barrier, len(peers))
-    for kv in range(2):
-        for which in range(2):
-            for n in range(2):
-                kv_copy(kv, n, which).start()
+
+    for kv in both:
+        for which in both:
+            @pl.when(has_next)
+            def _():
+                kv_next(kv, which).start()
+
+            @pl.when(first_core)
+            def _():
+                kv_mate(kv, which).start()
+
+    @pl.when(chip == 0)
+    def _():
+        keys[far, :] = jnp.zeros((ROWS, 2 * HD), BF16)
+        values[far, :] = jnp.zeros((ROWS, 2 * HD), BF16)
+
+    @pl.when(seq == 0)
+    def _():
+        keys[near, :] = jnp.zeros((ROWS, 2 * HD), BF16)
+        values[near, :] = jnp.zeros((ROWS, 2 * HD), BF16)
+
+    @pl.when(second_core)
+    def _():
+        halo_in[:, 0] = jnp.zeros((2, 2, HD, ROWS), BF16)
+
+    @pl.when(chip == 7)
+    def _():
+        halo_in[:, 1] = jnp.zeros((2, 2, HD, ROWS), BF16)
+
+    for n in (5, 6, 7):
+        load(n).start()
 
     load(4).wait()
 
@@ -150,8 +211,6 @@
         return carry
 
     lax.fori_loop(0, D // 256, transpose, 0)
-    for j in range(8):
-        mate_x(j).start()
 
     first_row = seq * ROWS
     dk_acc[...] = jnp.zeros_like(dk_acc)
@@ -173,8 +232,7 @@
         q2 = jnp.concatenate([q[rows, h] for h in heads], axis=0)
         g2 = jnp.concatenate([g[rows, h] for h in heads], axis=0)
         k, v = keys[span, lanes], values[span, lanes]
-        both = jnp.concatenate([bias[b], bias[b]], axis=0)
-        scores = dot(q2, k, NT) + both
+        scores = dot(q2, k, NT) + jnp.concatenate([bias[b], bias[b]], axis=0)
         top = jnp.max(scores, axis=1, keepdims=True)
         weight = jnp.exp2((scores - top) * EXP2_SCALE)
         probs = weight * (1.0 / jnp.sum(weight, axis=1, keepdims=True))
@@ -188,24 +246,79 @@
         dk_acc[kv, :, span] += dot(q2.T, score_low, NN)
         dv_acc[kv, :, span] += dot(g2.T, low, NN)
 
-    for kv in range(2):
-        for which in range(2):
-            for n in range(2):
-                kv_copy(kv, n, which).wait_recv()
-
-        def pair(b, carry, kv=kv):
-            attend(kv, 2 * b)
-            attend(kv, 2 * b + 1)
-            return carry
-
-        lax.fori_loop(0, ROWS // BLOCK // 2, pair, 0)
+    def kv_ready(kv):
+        @pl.when(first_core & has_prev)
+        def _():
+            for which in both:
+                kv_arrived(kv, 1, which)
+                kv_share(kv, which).start()
+            for which in both:
+                kv_arrived(kv, 0, which)
+
+        @pl.when(second_core)
+        def _():
+            for which in both:
+                kv_arrived(kv, 1, which)
+
+        @pl.when(second_core & has_prev)
+        def _():
+            for which in both:
+                kv_arrived(kv, 0, which)
+
+    def to_prev(kv, n):
+        for which in both:
+            grad_prev(kv, n, which).start()
+
+    def grads_out(kv):
         for n in (1, 0):
             cols = slice(WINDOW - (n + 1) * ROWS, WINDOW - n * ROWS)
             halo_out[kv, n, 0] = (dk_acc[kv, :, cols] * SCALE).astype(BF16)
             halo_out[kv, n, 1] = dv_acc[kv, :, cols].astype(BF16)
-            for which in range(2):
-                grad_copy(kv, n, which).start()
+
+            if n == 1:
+                @pl.when(second_core & has_prev)
+                def _():
+                    for which in both:
+                        grad_mate(kv, 1, which).start()
+
+                @pl.when(first_core & has_prev)
+                def _():
+                    to_prev(kv, 1)
+            else:
+                @pl.when(second_core)
+                def _():
+                    for which in both:
+                        grad_mate(kv, 0, which).start()
+
+    def grads_joined(kv):
+        @pl.when(first_core & has_prev)
+        def _():
+            for which in both:
+                grad_mate(kv, 1, which).wait_recv()
+                term = halo_out[kv, 0, which].astype(F32) + mate_far[kv, which].astype(F32)
+                halo_out[kv, 0, which] = term.astype(BF16)
+            to_prev(kv, 0)
+
+    for kv in both:
+        kv_ready(kv)
+        if kv == 0:
+            for j in range(8):
+                mate_x(j).start()
+
+        def pair(b, carry, kv=kv):
+            if kv == 1:
+                @pl.when(b == 1)
+                def _():
+                    grads_joined(0)
+
+            attend(kv, 2 * b)
+            attend(kv, 2 * b + 1)
+            return carry
+
+        lax.fori_loop(0, ROWS // BLOCK // 2, pair, 0)
+        grads_out(kv)
         mate_dq(kv).start()
+    grads_joined(1)
 
     def hop(axis, unit, n, src, dst, device):
         return remote(src, dst, send_sem.at[axis, unit, n], recv_sem.at[axis, unit, n], device)
@@ -232,22 +345,23 @@
     def crossing(axis, unit, way):
         rows = WAY_ROWS[way]
         slot = unit // 2 if axis == WEIGHT else unit
-        src = part.at[axis, unit, 3, rows]
-        if axis == WEIGHT:
-            return hop(axis, unit, 6 + way, src, zrelay.at[slot, rows], (above, below)[way])
-        return hop(axis, unit, 6 + way, src, zland.at[axis, slot, rows], beside)
-
-    def onward(unit, way):
-        rows = WAY_ROWS[way]
-        slot = unit // 2
-        return hop(
-            WEIGHT, unit, 8 + way, zrelay.at[slot, rows], zland.at[WEIGHT, slot, rows], (above, below)[way]
-        )
+        return hop(axis, unit, 6 + way, part.at[axis, unit, 3, rows], zland.at[axis, slot, rows], across[axis])
 
     def target(axis, side, u):
         off = 2 - u + (u // 2) * 3 - (u // 3) * 2
         z = (1 - depth[axis] + side) % 2
         return z * 4 + (place[axis] + off) % 4
+
+    def eager(axis, unit, u):
+        @pl.when(u == 0)
+        def _():
+            for way in both:
+                opposite(axis, unit, way).start()
+
+        for way in both:
+            @pl.when(u == 1 + way)
+            def _():
+                plain(axis, unit, way).start()
 
     def make_weight(unit):
         side, half = unit % 2, unit // 2
@@ -270,6 +384,8 @@
             product = dot(wq[j], dq[...], NT)
             product += dot(wkv[j], dkv[...], NN)
             part[INPUT, unit, u] = product.astype(BF16)
+            if unit == 0:
+                eager(INPUT, unit, u)
             return carry
 
         lax.fori_loop(0, 4, body, 0)
@@ -300,20 +416,12 @@
         for way in range(2):
             crossing(axis, unit, way).start()
 
-    def carry_on(unit):
-        for way in range(2):
-            crossing(WEIGHT, unit, way).wait_recv()
-            onward(unit, way).start()
-
     def finished(axis, unit):
         total = collected(axis, unit)
         source = unit - 1 if axis == WEIGHT else unit - 2
         slot = source // 2 if axis == WEIGHT else source
         for way in range(2):
-            if axis == WEIGHT:
-                onward(source, way).wait_recv()
-            else:
-                crossing(axis, source, way).wait_recv()
+            crossing(axis, source, way).wait_recv()
         return (total + zland[axis, slot].astype(F32)).astype(BF16)
 
     for j in range(8):
@@ -321,17 +429,22 @@
     for kv in range(2):
         mate_dq(kv).wait_recv()
     make_weight(0)
-    send(WEIGHT, 0)
+    opposite(WEIGHT, 0, 0).start()
+    plain(WEIGHT, 0, 0).start()
     make_weight(1)
-    forward(WEIGHT, 0)
-    send(WEIGHT, 1)
-
-    for kv in range(2):
-        for n in range(2):
-            for which in range(2):
-                grad_copy(kv, n, which).wait_recv()
-        own = slice(WINDOW, EXT)
-        halo = [halo_in[kv, 0, n].astype(F32) + halo_in[kv, 1, n].astype(F32) for n in range(2)]
+
+    own = slice(WINDOW, EXT)
+    for kv in both:
+        for which in both:
+            @pl.when(first_core)
+            def _():
+                grad_mate(kv, 0, which).wait_recv()
+
+            @pl.when(has_next)
+            def _():
+                grad_prev(kv, 0, which).wait_recv()
+
+        halo = [halo_in[kv, 0, n].astype(F32) + halo_in[kv, 1, n].astype(F32) for n in both]
         dkv[kv * HD:(kv + 1) * HD, :] = (dk_acc[kv, :, own] * SCALE + halo[0]).astype(BF16)
         dkv[(2 + kv) * HD:(3 + kv) * HD, :] = (dv_acc[kv, :, own] + halo[1]).astype(BF16)
     mate_dkv().start()
@@ -339,42 +452,65 @@
         load(n).wait()
 
     make_input(0)
-    send(INPUT, 0)
+    opposite(WEIGHT, 0, 1).start()
+    plain(WEIGHT, 0, 1).start()
     make_input(1)
-    forward(WEIGHT, 1)
+    mate_dkv().wait_recv()
+    make_weight(2)
     forward(INPUT, 0)
     send(INPUT, 1)
-    mate_dkv().wait_recv()
-    make_weight(2)
-    send(WEIGHT, 2)
+    forward(WEIGHT, 0)
+    send(WEIGHT, 1)
     make_input(2)
+    make_weight(3)
+    make_input(3)
+    cross(INPUT, 0)
     cross(WEIGHT, 0)
     forward(INPUT, 1)
     send(INPUT, 2)
-    make_weight(3)
+    forward(WEIGHT, 1)
+    send(WEIGHT, 2)
+    cross(INPUT, 1)
+    forward(INPUT, 2)
+    send(INPUT, 3)
     forward(WEIGHT, 2)
     send(WEIGHT, 3)
-    make_input(3)
-    carry_on(0)
-    cross(INPUT, 0)
-    forward(INPUT, 2)
-    send(INPUT, 3)
+    cross(WEIGHT, 2)
+    out_q[...] = finished(WEIGHT, 1)
+    forward(INPUT, 3)
     forward(WEIGHT, 3)
-    cross(WEIGHT, 2)
-    cross(INPUT, 1)
-    carry_on(2)
-    forward(INPUT, 3)
-    out_q[...] = finished(WEIGHT, 1)
-    out_kv[...] = finished(WEIGHT, 3)
     out_h[:PIECE, :] = finished(INPUT, 2)
     out_h[PIECE:, :] = finished(INPUT, 3)
-
-    for kv in range(2):
+    out_kv[...] = finished(WEIGHT, 3)
+
+    for kv in both:
         mate_dq(kv).wait_send()
-        for n in range(2):
-            for which in range(2):
-                kv_copy(kv, n, which).wait_send()
-                grad_copy(kv, n, which).wait_send()
+        for which in both:
+            @pl.when(has_next)
+            def _():
+                kv_next(kv, which).wait_send()
+
+            @pl.when(first_core)
+            def _():
+                kv_mate(kv, which).wait_send()
+
+            @pl.when(first_core & has_prev)
+            def _():
+                kv_share(kv, which).wait_send()
+
+            @pl.when(second_core)
+            def _():
+                grad_mate(kv, 0, which).wait_send()
+
+            @pl.when(second_core & has_prev)
+            def _():
+                grad_mate(kv, 1, which).wait_send()
+
+            @pl.when(first_core & has_prev)
+            def _():
+                grad_prev(kv, 0, which).wait_send()
+                grad_prev(kv, 1, which).wait_send()
+
     for j in range(8):
         mate_x(j).wait_send()
     mate_dkv().wait_send()
@@ -386,7 +522,6 @@
                 summed(axis, unit, way).wait_send()
                 if axis == WEIGHT and unit % 2 == 0:
                     crossing(axis, unit, way).wait_send()
-                    onward(unit, way).wait_send()
                 if axis == INPUT and unit < 2:
                     crossing(axis, unit, way).wait_send()
 
@@ -424,20 +559,20 @@
             pltpu.VMEM((COLS, ROWS), BF16),
             pltpu.VMEM((2, 2, 2, HD, ROWS), BF16),
             pltpu.VMEM((2, 2, 2, HD, ROWS), BF16),
+            pltpu.VMEM((2, 2, HD, ROWS), BF16),
             pltpu.VMEM((2, 4, 4) + piece, BF16),
             pltpu.VMEM((2, 4) + piece, BF16),
             pltpu.VMEM((2, 4, 2) + piece, BF16),
             pltpu.VMEM((2, 2) + piece, BF16),
-            pltpu.VMEM((2,) + piece, BF16),
             dma((8,)),
+            dma((2, 3, 2)),
             dma((2, 2, 2)),
             dma((2, 2, 2)),
-            dma((2, 2, 2)),
-            dma((2, 2, 2)),
+            dma((2, 3, 2)),
             dma((11,)),
             dma((11,)),
-            dma((2, 4, 10)),
-            dma((2, 4, 10)),
+            dma((2, 4, 8)),
+            dma((2, 4, 8)),
         ],
         compiler_params=pltpu.CompilerParams(
             collective_id=1, has_side_effects=True, vmem_limit_bytes=67043328
@@ -447,7 +582,7 @@
 
 
 def write_kernel(h, q, kv, out_h, out_q, out_k, out_v):
-    out_h[...] = h[...].T
+    out_h[...] = h[...]
     out_q[...] = q[...]
     out_k[...] = kv[:, : 2 * HD]
     out_v[...] = kv[:, 2 * HD:]
@@ -455,7 +590,7 @@
 
 def written(h, q, kv):
     vmem = pl.BlockSpec(memory_space=pltpu.VMEM)
-    shapes = ((ROWS, 2 * PIECE), (PIECE, COLS), (PIECE, COLS // 2), (PIECE, COLS // 2))
+    shapes = ((2 * PIECE, ROWS), (PIECE, COLS), (PIECE, COLS // 2), (PIECE, COLS // 2))
     return pl.pallas_call(
         write_kernel,
         out_shape=[jax.ShapeDtypeStruct(shape, BF16) for shape in shapes],
@@ -467,7 +602,9 @@
 
 def on_device(layer_input, query, keys, values, out_grad, w_query, w_key, w_value, proof_lengths):
     weights = [w.reshape(16, PIECE, -1) for w in (w_query, w_key, w_value)]
-    return tuple(written(*whole_step(proof_lengths, layer_input, query, out_grad, keys, values, *weights)))
+    results = whole_step(proof_lengths, layer_input, query, out_grad, keys, values, *weights)
+    input_grad, wq_grad, wk_grad, wv_grad = written(*results)
+    return (input_grad.T, wq_grad, wk_grad, wv_grad)
 
 
 def solution(mesh):

time: 106 us -> 89.9 us (0.85)
  the two profiles are of different devices: /device:TPU:6 before, /device:TPU:1 now
where the time goes in v3:
time: 89.9 us; the launch traced here: 89.8 us
  Pallas kernels  89.1 us (99%)
    pallas_call x1, Pallas kernels, whole_step(): pl.pallas_call(step_kernel, out_shape=[jax.ShapeDtypeStruct((2 * PIECE, R...  86.7 us
    pallas_call x1, Pallas kernels, written(): pl.pallas_call(write_kernel, out_shape=[jax.ShapeDtypeStruct(shape, BF16)...  2.38 us

profile of v3, /device:TPU:1, one launch (start us, length us, event | category | flops | bytes accessed | tf_op | source)
XLA Modules:
  0.0 89.8 jit_solution(6773579544204861178)
XLA Ops:
  0.6 86.7 %step.1 = (bf16[672,512]{1,0:T(8,128)(2,1)}, bf16[336,512]{1,0:T(8,128)(2,1)}, bf16[336,512]{1,0:T(8,128)(2,1)}) custom-call(s32[16]{0:T(128)} %lengths.1, bf16[512,5376]{1,0:T(8,128)(2,1)} %x.1, bf16[512,512]{1,0:T(8,128)(2,1)} %q_in.1, bf16[512,512]{1,0:T(8,128)(2,1)} %g_in.1, bf16[512,256]{1,0:T(8,128)(2,1)} %k_in.1, bf16[512,256]{1,0:T(8,128)(2,1)} %v_in.1, ...), custom_call_target="tpu_custom_call" | custom-call | tf_op jit(solution)/shard_map/step/pallas_call | solution.py:534
  87.4 2.4 %write.1 = (bf16[672,512]{1,0:T(8,128)(2,1)}, bf16[336,512]{1,0:T(8,128)(2,1)}, bf16[336,256]{1,0:T(8,128)(2,1)}, bf16[336,256]{1,0:T(8,128)(2,1)}) custom-call(bf16[672,512]{1,0:T(8,128)(2,1)} %get-tuple-element.11.h, bf16[336,512]{1,0:T(8,128)(2,1)} %get-tuple-element.12.q, bf16[336,512]{1,0:T(8,128)(2,1)} %get-tuple-element.13.kv), custom_call_target="tpu_custom_call" | custom-call | tf_op jit(solution)/shard_map/write/pallas_call | solution.py:594

commit v4 on v3

--- a/solution.py
+++ b/solution.py
@@ -20,7 +20,7 @@
 F32 = jnp.float32
 BF16 = jnp.bfloat16
 PIECE = 336
-CUT = 176
+CUTS = (176, 176)
 COLS = 512
 MESH = pl.DeviceIdType.MESH
 
@@ -28,7 +28,8 @@
 NT = (((1,), (1,)), ((), ()))
 
 WEIGHT, INPUT = 0, 1
-WAY_ROWS = (slice(0, CUT), slice(CUT, PIECE))
+WAY_ROWS = [(slice(0, cut), slice(cut, PIECE)) for cut in CUTS]
+HALF = COLS // 2
 
 
 def dot(left, right, dims):
@@ -55,9 +56,9 @@
     out_h, out_q, out_kv,
     x_nat, xt, x_mate, q, g, keys, values, wq, wkv, bias, dk_acc, dv_acc,
     dq, dq_mate, dkv, dkv_mate, halo_out, halo_in, mate_far,
-    part, relay, final, zland,
+    part, relay, final, zland, zfirst,
     load_sem, kv_send, kv_recv, gh_send, gh_recv, mate_send, mate_recv,
-    send_sem, recv_sem,
+    send_sem, recv_sem, early_send, early_recv,
 ):
     seq = lax.axis_index("seq")
     head = lax.axis_index("head")
@@ -323,29 +324,43 @@
     def hop(axis, unit, n, src, dst, device):
         return remote(src, dst, send_sem.at[axis, unit, n], recv_sem.at[axis, unit, n], device)
 
+    def lanes_of(axis, unit):
+        return slice(0, HALF) if (axis, unit) == (INPUT, 1) else slice(0, COLS)
+
     def opposite(axis, unit, way):
         device = (right, left)[way][axis]
-        rows = WAY_ROWS[way]
-        return hop(axis, unit, way, part.at[axis, unit, 0, rows], relay.at[axis, unit, rows], device)
+        rows, cols = WAY_ROWS[axis][way], lanes_of(axis, unit)
+        return hop(axis, unit, way, part.at[axis, unit, 0, rows, cols], relay.at[axis, unit, rows, cols], device)
 
     def plain(axis, unit, way):
         device = (right, left)[way][axis]
-        rows = WAY_ROWS[1 - way]
+        rows, cols = WAY_ROWS[axis][1 - way], lanes_of(axis, unit)
         return hop(
-            axis, unit, 2 + way, part.at[axis, unit, 1 + way, rows], final.at[axis, unit, way, rows], device
+            axis, unit, 2 + way, part.at[axis, unit, 1 + way, rows, cols], final.at[axis, unit, way, rows, cols], device
         )
 
     def summed(axis, unit, way):
         device = (right, left)[way][axis]
-        rows = WAY_ROWS[way]
+        rows, cols = WAY_ROWS[axis][way], lanes_of(axis, unit)
         return hop(
-            axis, unit, 4 + way, part.at[axis, unit, 1 + way, rows], final.at[axis, unit, way, rows], device
+            axis, unit, 4 + way, part.at[axis, unit, 1 + way, rows, cols], final.at[axis, unit, way, rows, cols], device
         )
 
     def crossing(axis, unit, way):
-        rows = WAY_ROWS[way]
+        rows, cols = WAY_ROWS[axis][way], lanes_of(axis, unit)
         slot = unit // 2 if axis == WEIGHT else unit
-        return hop(axis, unit, 6 + way, part.at[axis, unit, 3, rows], zland.at[axis, slot, rows], across[axis])
+        return hop(axis, unit, 6 + way, part.at[axis, unit, 3, rows, cols], zland.at[axis, slot, rows, cols], across[axis])
+
+    def early(u):
+        return remote(
+            part.at[INPUT, 1, u, :, HALF:], zfirst.at[u], early_send.at[u], early_recv.at[u], across[INPUT]
+        )
+
+    def join_early():
+        for u in range(4):
+            early(u).wait_recv()
+            kept = part[INPUT, 3, u, :, HALF:].astype(F32)
+            part[INPUT, 3, u, :, HALF:] = (kept + zfirst[u].astype(F32)).astype(BF16)
 
     def target(axis, side, u):
         off = 2 - u + (u // 2) * 3 - (u // 3) * 2
@@ -397,32 +412,38 @@
             plain(axis, unit, way).start()
 
     def forward(axis, unit):
+        cols = lanes_of(axis, unit)
         for way in range(2):
             opposite(axis, unit, way).wait_recv()
-            rows = WAY_ROWS[way]
-            kept = part[axis, unit, 1 + way, rows].astype(F32)
-            part[axis, unit, 1 + way, rows] = (kept + relay[axis, unit, rows].astype(F32)).astype(BF16)
+            rows = WAY_ROWS[axis][way]
+            kept = part[axis, unit, 1 + way, rows, cols].astype(F32)
+            kept += relay[axis, unit, rows, cols].astype(F32)
+            part[axis, unit, 1 + way, rows, cols] = kept.astype(BF16)
             summed(axis, unit, way).start()
 
     def collected(axis, unit):
+        cols = lanes_of(axis, unit)
         for way in range(2):
             plain(axis, unit, way).wait_recv()
             summed(axis, unit, way).wait_recv()
-        total = part[axis, unit, 3].astype(F32)
-        return total + final[axis, unit, 0].astype(F32) + final[axis, unit, 1].astype(F32)
+        total = part[axis, unit, 3, :, cols].astype(F32)
+        return total + final[axis, unit, 0, :, cols].astype(F32) + final[axis, unit, 1, :, cols].astype(F32)
 
     def cross(axis, unit):
-        part[axis, unit, 3] = collected(axis, unit).astype(BF16)
+        part[axis, unit, 3, :, lanes_of(axis, unit)] = collected(axis, unit).astype(BF16)
         for way in range(2):
             crossing(axis, unit, way).start()
 
-    def finished(axis, unit):
+    def finish(axis, unit, out):
         total = collected(axis, unit)
         source = unit - 1 if axis == WEIGHT else unit - 2
         slot = source // 2 if axis == WEIGHT else source
+        cols = lanes_of(axis, source)
         for way in range(2):
             crossing(axis, source, way).wait_recv()
-        return (total + zland[axis, slot].astype(F32)).astype(BF16)
+        out[:, cols] = (total[:, cols] + zland[axis, slot, :, cols].astype(F32)).astype(BF16)
+        if cols.stop < COLS:
+            out[:, HALF:] = total[:, HALF:].astype(BF16)
 
     for j in range(8):
         mate_x(j).wait_recv()
@@ -455,12 +476,14 @@
     opposite(WEIGHT, 0, 1).start()
     plain(WEIGHT, 0, 1).start()
     make_input(1)
+    for u in range(4):
+        early(u).start()
     mate_dkv().wait_recv()
     make_weight(2)
     forward(INPUT, 0)
     send(INPUT, 1)
     forward(WEIGHT, 0)
-    send(WEIGHT, 1)
+    send(WEIGHT, 2)
     make_input(2)
     make_weight(3)
     make_input(3)
@@ -468,20 +491,21 @@
     cross(WEIGHT, 0)
     forward(INPUT, 1)
     send(INPUT, 2)
-    forward(WEIGHT, 1)
-    send(WEIGHT, 2)
+    forward(WEIGHT, 2)
+    send(WEIGHT, 1)
     cross(INPUT, 1)
+    join_early()
     forward(INPUT, 2)
     send(INPUT, 3)
-    forward(WEIGHT, 2)
+    cross(WEIGHT, 2)
+    forward(WEIGHT, 1)
     send(WEIGHT, 3)
-    cross(WEIGHT, 2)
-    out_q[...] = finished(WEIGHT, 1)
     forward(INPUT, 3)
     forward(WEIGHT, 3)
-    out_h[:PIECE, :] = finished(INPUT, 2)
-    out_h[PIECE:, :] = finished(INPUT, 3)
-    out_kv[...] = finished(WEIGHT, 3)
+    finish(WEIGHT, 1, out_q)
+    finish(INPUT, 2, out_h.at[:PIECE])
+    finish(INPUT, 3, out_h.at[PIECE:])
+    finish(WEIGHT, 3, out_kv)
 
     for kv in both:
         mate_dq(kv).wait_send()
@@ -514,6 +538,8 @@
     for j in range(8):
         mate_x(j).wait_send()
     mate_dkv().wait_send()
+    for u in range(4):
+        early(u).wait_send()
     for axis in range(2):
         for unit in range(4):
             for way in range(2):
@@ -564,6 +590,7 @@
             pltpu.VMEM((2, 4) + piece, BF16),
             pltpu.VMEM((2, 4, 2) + piece, BF16),
             pltpu.VMEM((2, 2) + piece, BF16),
+            pltpu.VMEM((4, PIECE, HALF), BF16),
             dma((8,)),
             dma((2, 3, 2)),
             dma((2, 2, 2)),
@@ -573,6 +600,8 @@
             dma((11,)),
             dma((2, 4, 8)),
             dma((2, 4, 8)),
+            dma((4,)),
+            dma((4,)),
         ],
         compiler_params=pltpu.CompilerParams(
             collective_id=1, has_side_effects=True, vmem_limit_bytes=67043328
@@ -581,21 +610,42 @@
     )(lengths, x, q, g, k, v, wq, wk, wv)
 
 
-def write_kernel(h, q, kv, out_h, out_q, out_k, out_v):
-    out_h[...] = h[...]
-    out_q[...] = q[...]
-    out_k[...] = kv[:, : 2 * HD]
-    out_v[...] = kv[:, 2 * HD:]
+def write_kernel(h, q, kv, out_h, out_q, out_k, out_v, h_at, q_at, kv_at, read, write):
+    loads = [
+        pltpu.make_async_copy(src, dst, read.at[n])
+        for n, (src, dst) in enumerate(((h, h_at), (q, q_at), (kv, kv_at)))
+    ]
+    stores = [
+        pltpu.make_async_copy(src, dst, write.at[n])
+        for n, (src, dst) in enumerate((
+            (h_at, out_h), (q_at, out_q), (kv_at.at[:, :HALF], out_k), (kv_at.at[:, HALF:], out_v),
+        ))
+    ]
+    for copy in loads:
+        copy.start()
+    for n, needs in enumerate((0, 1, 2, None)):
+        if needs is not None:
+            loads[needs].wait()
+        stores[n].start()
+    for copy in stores:
+        copy.wait()
 
 
 def written(h, q, kv):
-    vmem = pl.BlockSpec(memory_space=pltpu.VMEM)
+    anywhere = pl.BlockSpec(memory_space=pl.ANY)
     shapes = ((2 * PIECE, ROWS), (PIECE, COLS), (PIECE, COLS // 2), (PIECE, COLS // 2))
     return pl.pallas_call(
         write_kernel,
         out_shape=[jax.ShapeDtypeStruct(shape, BF16) for shape in shapes],
-        in_specs=[vmem] * 3,
-        out_specs=[vmem] * 4,
+        in_specs=[anywhere] * 3,
+        out_specs=[anywhere] * 4,
+        scratch_shapes=[
+            pltpu.VMEM((2 * PIECE, ROWS), BF16),
+            pltpu.VMEM((PIECE, COLS), BF16),
+            pltpu.VMEM((PIECE, COLS), BF16),
+            pltpu.SemaphoreType.DMA((3,)),
+            pltpu.SemaphoreType.DMA((4,)),
+        ],
         name="write",
     )(h, q, kv)
 

time: 89.9 us -> 89 us (0.990)
  Pallas kernels: 89.1 us -> 88.2 us
where the time goes in v4:
time: 89 us; the launch traced here: 88.9 us
  Pallas kernels  88.2 us (99%)
    pallas_call x1, Pallas kernels, whole_step(): pl.pallas_call(step_kernel, out_shape=[jax.ShapeDtypeStruct((2 * PIECE, R...  86 us
    pallas_call x1, Pallas kernels, written(): pl.pallas_call(write_kernel, out_shape=[jax.ShapeDtypeStruct(shape, BF16)...  2.23 us

profile of v4, /device:TPU:1, one launch (start us, length us, event | category | flops | bytes accessed | tf_op | source)
XLA Modules:
  0.0 88.9 jit_solution(1131445896096604664)
XLA Ops:
  0.6 86.0 %step.1 = (bf16[672,512]{1,0:T(8,128)(2,1)}, bf16[336,512]{1,0:T(8,128)(2,1)}, bf16[336,512]{1,0:T(8,128)(2,1)}) custom-call(s32[16]{0:T(128)} %lengths.1, bf16[512,5376]{1,0:T(8,128)(2,1)} %x.1, bf16[512,512]{1,0:T(8,128)(2,1)} %q_in.1, bf16[512,512]{1,0:T(8,128)(2,1)} %g_in.1, bf16[512,256]{1,0:T(8,128)(2,1)} %k_in.1, bf16[512,256]{1,0:T(8,128)(2,1)} %v_in.1, ...), custom_call_target="tpu_custom_call" | custom-call | tf_op jit(solution)/shard_map/step/pallas_call | solution.py:560
  86.7 2.2 %write.1 = (bf16[672,512]{1,0:T(8,128)(2,1)}, bf16[336,512]{1,0:T(8,128)(2,1)}, bf16[336,256]{1,0:T(8,128)(2,1)}, bf16[336,256]{1,0:T(8,128)(2,1)}) custom-call(bf16[672,512]{1,0:T(8,128)(2,1)} %get-tuple-element.11.h, bf16[336,512]{1,0:T(8,128)(2,1)} %get-tuple-element.12.q, bf16[336,512]{1,0:T(8,128)(2,1)} %get-tuple-element.13.kv), custom_call_target="tpu_custom_call" | custom-call | tf_op jit(solution)/shard_map/write/pallas_call | solution.py:637
